TPU v7x, 256 devices: a whole 4x4x8 slice. The times are simulated.
256 devices in a mesh: dp: 32 (over x, z_hi, core), expert: 8 (over y, z_lo).
Axes of the slice: x: 4, y: 4, z: 8 (z_hi: 4, z_lo: 2; z = z_hi * 2 + z_lo), core: 2. Of those that a mesh axis runs over, the one named last changes fastest.
Arguments:
- tokens: bfloat16 [32768, 4096], P(('dp', 'expert')), may hold values from -6 to 6
- cotangent: bfloat16 [32768, 4096], P(('dp', 'expert')), may hold values from -1.1953125 to 1.1953125
- expert_ids: int32 [32768, 2], P(('dp', 'expert')), may hold values from 0 to 63, as said below
- gate_probs: bfloat16 [32768, 2], P(('dp', 'expert')), may hold values from 0.049804688 to 1
- gate_w: bfloat16 [8, 7168, 4096], P('expert', 'dp'), may hold values from -0.09375 to 0.09375
- up_w: bfloat16 [8, 7168, 4096], P('expert', 'dp'), may hold values from -0.09375 to 0.09375
- down_w: bfloat16 [8, 7168, 4096], P('expert', 'dp'), may hold values from -0.0625 to 0.0625
Outputs:
- grad_gate: bfloat16 [8, 7168, 4096], P('expert', 'dp')
- grad_up: bfloat16 [8, 7168, 4096], P('expert', 'dp')
- grad_down: bfloat16 [8, 7168, 4096], P('expert', 'dp')
- grad_probs: float32 [32768, 2], P(('dp', 'expert'))
Inputs may be any that keep to these rules, and one draw needn't show every extreme that they name: `expert_ids`: each token names two different experts. Split the rows into aligned blocks of 128 (the rows of one device) and those into aligned runs of 8 blocks: a block names any one expert below 8 at most 4 times, and a run names it at most 16 times; in every draw some block reaches 4 and some run reaches 16.
All inputs are finite; a program needn't handle non-finite values.
Results may differ from a plain program's by a relative error of at most 0.015.
Values may be sent and summed in bfloat16 or wider, within the bound.
No kernel may reach another device: no remote copies, remote signals or barrier semaphores. Data moves between devices by JAX's collectives and lax.ppermute only.
A program may use at most 128 MiB of HBM per device.

v0:
```python
import jax
import jax.numpy as jnp
from jax import lax
from jax.sharding import PartitionSpec as P

ROW_CAPACITY = 4


def contract_rows(left, right):
    return lax.dot_general(
        left, right, (((0,), (0,)), ((), ())), preferred_element_type=jnp.float32
    )


def contract_cols(left, right):
    return lax.dot_general(
        left, right, (((1,), (1,)), ((), ())), preferred_element_type=jnp.float32
    )


def shards(tokens, cotangent, expert_ids, gate_probs, gate_w, up_w, down_w):
    owners = lax.axis_size("expert")
    slots = owners * ROW_CAPACITY
    flat_ids = expert_ids.reshape(-1)
    marks = (flat_ids[:, None] == jnp.arange(owners, dtype=jnp.int32)[None, :]).astype(jnp.int32)
    before = jnp.cumsum(marks, axis=0) - marks
    ranking = jnp.sum(before * marks, axis=1)
    target = jnp.where(jnp.sum(marks, axis=1) > 0, flat_ids * ROW_CAPACITY + ranking, -1)
    routing = (target[None, :] == jnp.arange(slots, dtype=jnp.int32)[:, None]).astype(jnp.float32)
    per_token = routing.reshape(slots, -1, 2).sum(axis=2).astype(jnp.bfloat16)
    send_x = jnp.dot(per_token, tokens, preferred_element_type=jnp.float32).astype(jnp.bfloat16)
    send_dy = jnp.dot(per_token, cotangent, preferred_element_type=jnp.float32).astype(jnp.bfloat16)
    send_p = jnp.dot(
        routing.astype(jnp.bfloat16), gate_probs.reshape(-1), preferred_element_type=jnp.float32
    ).astype(jnp.bfloat16)
    got_x, got_dy, got_p = (
        lax.all_to_all(
            send_x.reshape(owners, ROW_CAPACITY, -1),
            "expert",
            split_axis=0,
            concat_axis=0,
            tiled=True,
        ),
        lax.all_to_all(
            send_dy.reshape(owners, ROW_CAPACITY, -1),
            "expert",
            split_axis=0,
            concat_axis=0,
            tiled=True,
        ),
        lax.all_to_all(
            send_p.reshape(owners, ROW_CAPACITY), "expert", split_axis=0, concat_axis=0, tiled=True
        ),
    )
    rows_x = got_x.reshape(slots, -1)
    rows_dy = got_dy.reshape(slots, -1)
    rows_p = got_p.reshape(slots)
    gate_local = gate_w[0]
    up_local = up_w[0]
    down_local = down_w[0]
    piece_x = lax.all_gather(rows_x, "dp", axis=0, tiled=True)
    piece_dy = lax.all_gather(rows_dy, "dp", axis=0, tiled=True)
    piece_p = lax.all_gather(rows_p, "dp", axis=0, tiled=True)
    weight_p = piece_p.astype(jnp.float32)[:, None]
    gate_pre = contract_cols(piece_x, gate_local)
    up_pre = contract_cols(piece_x, up_local)
    sigma = jax.nn.sigmoid(gate_pre)
    hidden = (gate_pre * sigma * up_pre).astype(jnp.bfloat16)
    pulled = contract_cols(piece_dy, down_local)
    router = jnp.sum(hidden.astype(jnp.float32) * pulled, axis=1)
    scaled_dy = (weight_p * piece_dy.astype(jnp.float32)).astype(jnp.bfloat16)
    d_hidden = weight_p * pulled
    d_gate = (d_hidden * up_pre * sigma * (1.0 + gate_pre * (1.0 - sigma))).astype(jnp.bfloat16)
    d_up = (d_hidden * gate_pre * sigma).astype(jnp.bfloat16)
    new_gate = contract_rows(d_gate, piece_x)
    new_up = contract_rows(d_up, piece_x)
    new_down = contract_rows(hidden, scaled_dy)
    router_rows = lax.psum_scatter(router, "dp", scatter_dimension=0, tiled=True)
    returned = lax.all_to_all(
        router_rows.reshape(owners, ROW_CAPACITY), "expert", split_axis=0, concat_axis=0, tiled=True
    )
    grad_flat = jnp.dot(returned.reshape(slots), routing, precision=lax.Precision.HIGHEST)
    grad_gate = new_gate.astype(jnp.bfloat16)[None]
    grad_up = new_up.astype(jnp.bfloat16)[None]
    grad_down = new_down.astype(jnp.bfloat16)[None]
    return (grad_gate, grad_up, grad_down, grad_flat.reshape(-1, 2))


def solution(mesh):
    in_specs = (
        P(("dp", "expert"), None),
        P(("dp", "expert"), None),
        P(("dp", "expert"), None),
        P(("dp", "expert"), None),
        P("expert", "dp", None),
        P("expert", "dp", None),
        P("expert", "dp", None),
    )
    out_specs = (
        P("expert", "dp", None),
        P("expert", "dp", None),
        P("expert", "dp", None),
        P(("dp", "expert"), None),
    )
    return jax.shard_map(shards, mesh=mesh, in_specs=in_specs, out_specs=out_specs, check_vma=False)
```

profile of v0, /device:TPU:1, one launch (start us, length us, event | category | flops | bytes accessed | tf_op | source)
XLA Modules:
  0.0 296.1 jit_solution(5309269911778163074)
XLA Ops:
  7.2 0.0 copy-start
  7.2 0.0 all-gather.5.cloned.1.call-start
  7.2 0.9 copy.36
  8.1 0.1 eq.64
  8.3 0.1 eq.68
  8.4 0.6 reduce-window.6
  9.0 0.2 slice_reduce_fusion
  9.3 0.1 fusion.23
  9.4 0.1 reduce_sum.40
  9.5 0.2 gt.17
  9.7 0.1 copy.41
  9.8 0.1 copy.40
  9.8 0.7 add_select_fusion
  10.6 1.5 convolution_convert_fusion.2
  12.1 0.1 reshape.108
  12.2 12.4 %all_to_all.29 = bf16[8,4,4096]{2,1,0:T(4,128)(2,1)S(1)} all-to-all(bf16[8,4,4096]{2,1,0:T(4,128)(2,1)S(1)} %reshape.108), channel_id=1, replica_groups=mesh['dp'=32,'expert'=8] {'expert'}, dimensions={0} | all-to-all | bytes 524288 | tf_op jit(solution)/shard_map/all_to_all | solution.py:37
  24.5 0.8 reshape.109
  25.3 0.0 all-gather.5.cloned.1.call-update
  25.3 0.0 all-gather.3.cloned.1.call-start
  25.4 1.5 convolution_convert_fusion.3
  26.9 0.1 reshape.106
  27.0 8.5 %all_to_all.30 = bf16[8,4,4096]{2,1,0:T(4,128)(2,1)S(1)} all-to-all(bf16[8,4,4096]{2,1,0:T(4,128)(2,1)S(1)} %reshape.106), channel_id=1, replica_groups=mesh['dp'=32,'expert'=8] {'expert'}, dimensions={0} | all-to-all | bytes 524288 | tf_op jit(solution)/shard_map/all_to_all | solution.py:44
  35.5 0.8 reshape.107
  36.3 0.0 all-gather.3.cloned.1.call-update
  36.3 0.8 copy.38
  37.1 0.1 reshape.116
  37.3 0.1 fusion.12
  37.4 0.7 all_to_all.24
  38.1 3.3 %all-to-all-start = ((bf16[8,1,4]{2,1,0:T(2,128)(2,1)}), bf16[8,1,4]{2,1,0:T(2,128)(2,1)S(1)}, u32[]{:S(2)}, u32[]{:S(2)}) async-start(bf16[8,1,4]{2,1,0:T(2,128)(2,1)} %all_to_all.24), calls=%async_computation | async-start | bytes 8192 | tf_op jit(solution)/shard_map/all_to_all | solution.py:51
  41.4 1.3 fusion.29
  44.0 3.0 %all-to-all-done = bf16[8,1,4]{2,1,0:T(2,128)(2,1)S(1)} async-done(((bf16[8,1,4]{2,1,0:T(2,128)(2,1)}), bf16[8,1,4]{2,1,0:T(2,128)(2,1)S(1)}, u32[]{:S(2)}, u32[]{:S(2)}) %all-to-all-start) | async-done | bytes 96 | tf_op jit(solution)/shard_map/all_to_all | solution.py:51
  47.0 0.1 reshape.111
  47.1 0.2 dynamic-update-slice
  47.4 77.7 %all-reduce = bf16[1024]{0:T(1024)(128)(2,1)S(1)} all-reduce(bf16[1024]{0:T(1024)(128)(2,1)S(1)} %dynamic-update-slice), channel_id=1, replica_groups=mesh['dp'=32,'expert'=8] {'dp'}, use_global_device_ids=true, to_apply=%add | all-reduce | flops 1024 | bytes 4096
  125.1 0.0 all-gather.5.cloned.1.call-done
  125.1 0.0 copy-start.1
  125.2 0.0 copy-start.3
  125.2 6.8 %fusion.6 = f32[1024,224]{0,1:T(8,128)S(1)} fusion(bf16[1024,4096]{1,0:T(8,128)(2,1)} %all-gather.5.cloned.1.call-done, bf16[1,224,4096]{2,1,0:T(8,128)(2,1)} %param.11), kind=kOutput, calls=%fused_computation.11 | convolution fusion | flops 1879048192 | bytes 11141120 | tf_op jit(solution)/shard_map/dot_general | solution.py:16
  131.9 0.0 copy-done.1
  131.9 0.1 copy-done.3
  132.1 3.6 %fusion.8 = f32[1024,224]{0,1:T(8,128)} fusion(bf16[1024,4096]{1,0:T(8,128)(2,1)S(1)} %copy-done.1, bf16[1,224,4096]{2,1,0:T(8,128)(2,1)S(1)} %copy-done.3), kind=kOutput, calls=%fused_computation.13 | convolution fusion | flops 1879048192 | bytes 11141120 | tf_op jit(solution)/shard_map/dot_general | solution.py:16
  135.6 48.7 %all-gather.3.cloned.1.call-done = bf16[1024,4096]{1,0:T(8,128)(2,1)} async-done(((bf16[32,4096]{1,0:T(8,128)(2,1)}), bf16[1024,4096]{1,0:T(8,128)(2,1)}) %all-gather.3.cloned.1.call-update) | async-done | bytes 8388624 | tf_op jit(solution)/shard_map/all_gather | solution.py:62
  184.3 0.0 copy-done
  184.3 7.2 %multiply_reduce_fusion = (f32[1024]{0:T(1024)S(1)}, bf16[1024,224]{0,1:T(8,128)(2,1)S(1)}, f32[1024,224]{0,1:T(8,128)}) fusion(f32[1024,224]{0,1:T(8,128)} %fusion.8, f32[1024,224]{0,1:T(8,128)S(1)} %fusion.6, bf16[1024,4096]{1,0:T(8,128)(2,1)} %all-gather.3.cloned.1.call-done, bf16[1,224,4096]{2,1,0:T(8,128)(2,1)S(1)} %copy-done), kind=kOutput, calls=%fused_computation.19 | convolution fusion | flops 1881111552 | bytes 13438976 | tf_op jit(solution)/shard_map/dot_general | solution.py:16
  191.5 71.0 %all-reduce.1 = f32[1024]{0:T(1024)S(1)} all-reduce(f32[1024]{0:T(1024)S(1)} %get-tuple-element.6), channel_id=2, replica_groups=mesh['dp'=32,'expert'=8] {'dp'}, use_global_device_ids=true, to_apply=%region_6.7.clone | all-reduce | flops 1024 | bytes 8192
  262.6 0.1 dynamic-slice.2
  262.6 0.7 all_to_all.22
  263.3 6.0 %all-to-all-start.3 = ((f32[8,1,4]{2,1,0:T(1,128)}), f32[8,1,4]{2,1,0:T(1,128)S(1)}, u32[]{:S(2)}, u32[]{:S(2)}) async-start(f32[8,1,4]{2,1,0:T(1,128)} %bitcast.10), calls=%async_computation.3 | async-start | bytes 8192 | tf_op jit(solution)/shard_map/all_to_all | solution.py:79
  269.3 0.0 copy-start.4
  269.3 7.5 %fusion.3 = bf16[1,224,4096]{2,1,0:T(8,128)(2,1)} fusion(bf16[1024,4096]{1,0:T(8,128)(2,1)} %all-gather.5.cloned.1.call-done, f32[1024,224]{0,1:T(8,128)S(1)} %fusion.6, f32[1024,224]{0,1:T(8,128)} %fusion.8, f32[1024,224]{0,1:T(8,128)} %get-tuple-element.12, f32[1024]{0:T(1024)S(1)} %convert_element_type.63), kind=kOutput, calls=%fused_computation.6 | convolution fusion | flops 1882488832 | bytes 12980224 | tf_op jit(solution)/shard_map/dot_general | solution.py:10
  276.9 0.0 copy-done.4
  276.9 0.0 copy-start.2
  276.9 6.9 %fusion.4 = bf16[1,224,4096]{2,1,0:T(8,128)(2,1)} fusion(bf16[1024,4096]{1,0:T(8,128)(2,1)} %all-gather.5.cloned.1.call-done, f32[1024,224]{0,1:T(8,128)S(1)} %fusion.6, f32[1024,224]{0,1:T(8,128)S(1)} %copy-done.4, f32[1024]{0:T(1024)S(1)} %convert_element_type.63), kind=kOutput, calls=%fused_computation.7 | convolution fusion | flops 1881571328 | bytes 12062720 | tf_op jit(solution)/shard_map/dot_general | solution.py:10
  283.8 0.0 copy-done.2
  283.8 3.5 %fusion.5 = bf16[1,224,4096]{2,1,0:T(8,128)(2,1)} fusion(bf16[1024,224]{0,1:T(8,128)(2,1)S(1)} %get-tuple-element.7, bf16[1024,4096]{1,0:T(8,128)(2,1)S(1)} %copy-done.2, f32[1024]{0:T(1024)S(1)} %convert_element_type.63), kind=kOutput, calls=%fused_computation.8 | convolution fusion | flops 1892548608 | bytes 10686464 | tf_op jit(solution)/shard_map/dot_general | solution.py:10
  287.3 0.0 all-to-all-done.3
  287.3 0.5 broadcast.75
  287.8 0.7 reduce.6
  288.5 0.1 reshape.118
  288.6 0.7 fusion.18
  (8 shorter events, 0.1 us)
Async XLA Ops:
  7.2 177.2 %copy-start = (bf16[1,224,4096]{2,1,0:T(8,128)(2,1)S(1)}, bf16[1,224,4096]{2,1,0:T(8,128)(2,1)}, u32[]{:S(2)}) copy-start(bf16[1,224,4096]{2,1,0:T(8,128)(2,1)} %param.13) | copy-start | bytes 5505028
  7.2 118.0 %all-gather.5.cloned.1.call-start = ((), (), s32[]{:S(2)}) async-start(), calls=%async_computation.5 | async-start | bytes 8650752 | tf_op jit(solution)/shard_map/all_gather | solution.py:61
  25.3 159.0 %all-gather.3.cloned.1.call-start = ((), (), s32[]{:S(2)}) async-start(), calls=%async_computation.4 | async-start | bytes 8650752 | tf_op jit(solution)/shard_map/all_gather | solution.py:62
  38.1 8.9 %all-to-all-start = ((bf16[8,1,4]{2,1,0:T(2,128)(2,1)}), bf16[8,1,4]{2,1,0:T(2,128)(2,1)S(1)}, u32[]{:S(2)}, u32[]{:S(2)}) async-start(bf16[8,1,4]{2,1,0:T(2,128)(2,1)} %all_to_all.24), calls=%async_computation | async-start | bytes 8192 | tf_op jit(solution)/shard_map/all_to_all | solution.py:51
  125.1 6.8 %copy-start.1 = (bf16[1024,4096]{1,0:T(8,128)(2,1)S(1)}, bf16[1024,4096]{1,0:T(8,128)(2,1)}, u32[]{:S(2)}) copy-start(bf16[1024,4096]{1,0:T(8,128)(2,1)} %all-gather.5.cloned.1.call-done) | copy-start | bytes 25165828
  125.2 6.9 %copy-start.3 = (bf16[1,224,4096]{2,1,0:T(8,128)(2,1)S(1)}, bf16[1,224,4096]{2,1,0:T(8,128)(2,1)}, u32[]{:S(2)}) copy-start(bf16[1,224,4096]{2,1,0:T(8,128)(2,1)} %param.12) | copy-start | bytes 5505028
  263.3 24.0 %all-to-all-start.3 = ((f32[8,1,4]{2,1,0:T(1,128)}), f32[8,1,4]{2,1,0:T(1,128)S(1)}, u32[]{:S(2)}, u32[]{:S(2)}) async-start(f32[8,1,4]{2,1,0:T(1,128)} %bitcast.10), calls=%async_computation.3 | async-start | bytes 8192 | tf_op jit(solution)/shard_map/all_to_all | solution.py:79
  269.3 7.5 %copy-start.4 = (f32[1024,224]{0,1:T(8,128)S(1)}, f32[1024,224]{0,1:T(8,128)}, u32[]{:S(2)}) copy-start(f32[1024,224]{0,1:T(8,128)} %get-tuple-element.12) | copy-start | bytes 2752516
  276.9 6.9 %copy-start.2 = (bf16[1024,4096]{1,0:T(8,128)(2,1)S(1)}, bf16[1024,4096]{1,0:T(8,128)(2,1)}, u32[]{:S(2)}) copy-start(bf16[1024,4096]{1,0:T(8,128)(2,1)} %all-gather.3.cloned.1.call-done) | copy-start | bytes 25165828
Sparse Core Ops, SparseCore 0:
  25.5 78.6 all-gather.4
  107.3 77.0 all-gather.2
where the time goes:
time: 300 us; the launch traced here: 296 us
  blocking collectives  170 us (57%)
  waiting for transfers between devices  51.8 us (17%)
  matrix products  39.3 us (13%)
  between operations  15.4 us (5%)
  starting transfers between devices  9.42 us (3%)
  local copies, waits for them, and re-layouts  8.39 us (3%)
    unnamed x2, blocking collectives  149 us
    all_gather x1, waiting for transfers between devices, shards(): piece_dy = lax.all_gather(rows_dy, 'dp', axis=0, tiled=True)  48.7 us
    dot_general x3, matrix products, contract_rows(): lax.dot_general(left, right, (((0,), (0,)), ((), ())), preferred_element_...  17.9 us
    dot_general x3, matrix products, contract_cols(): lax.dot_general(left, right, (((1,), (1,)), ((), ())), preferred_element_...  17.5 us
    all_to_all x1, blocking collectives, shards(): lax.all_to_all(send_x.reshape(owners, ROW_CAPACITY, -1), 'expert', split_...  12.4 us
    all_to_all x1, blocking collectives, shards(): lax.all_to_all(send_dy.reshape(owners, ROW_CAPACITY, -1), 'expert', split...  8.55 us
    all_to_all x1, starting transfers between devices, shards(): lax.all_to_all(router_rows.reshape(owners, ROW_CAPACITY), 'expert', split...  6.02 us
  transfers between devices with their start and end apart: 4, of which 2 were waited for; matrix products, arithmetic and copies ran while one was open for 11% of the time, Pallas kernels for 0%

commit v1 on v0

v1 whole, which is shorter than its diff:
```python
import functools

import jax
import jax.numpy as jnp
from jax import lax
from jax.experimental import pallas as pl
from jax.experimental.pallas import tpu as pltpu
from jax.sharding import Mesh, PartitionSpec as P

CAP = 4
RECV = 16
BF = jnp.bfloat16
F32 = jnp.float32
I32 = jnp.int32
ALL = ("x", "zh", "c", "y", "zl")
SIZES = {"x": 4, "zh": 4, "c": 2, "y": 4, "zl": 2}
VMEM = pl.BlockSpec(memory_space=pltpu.VMEM)


def iota(shape, dim):
    return lax.broadcasted_iota(I32, shape, dim)


def nt(a, b, precision=None):
    return lax.dot_general(
        a, b, (((1,), (1,)), ((), ())), preferred_element_type=F32, precision=precision
    )


def nn(a, b):
    return lax.dot_general(a, b, (((1,), (0,)), ((), ())), preferred_element_type=F32)


def marks(ids):
    n = ids.shape[1]
    rows = iota((8, n), 0)
    first = ids[0:1, :] == rows
    second = ids[1:2, :] == rows
    hit = jnp.where(first | second, 1.0, 0.0).astype(F32)
    earlier = jnp.where(iota((n, n), 0) < iota((n, n), 1), 1.0, 0.0)
    before = nn(hit.astype(BF), earlier.astype(BF))
    return first, second, hit, before


def dispatch_kernel(ids_ref, p_ref, tok_ref, cot_ref, out_ref):
    d = tok_ref.shape[1]
    n = tok_ref.shape[0]
    me = lax.axis_index(ALL).astype(F32)
    first, _, hit, before = marks(ids_ref[...])
    p = p_ref[...].astype(F32)
    weight = jnp.where(first, p[0:1, :], p[1:2, :])
    spread = jnp.where(iota((8 * CAP, 8), 0) // CAP == iota((8 * CAP, 8), 1), 1.0, 0.0)
    spread = spread.astype(BF)
    hit = nn(spread, hit.astype(BF))
    before = nn(spread, before.astype(BF))
    weight = nn(spread, weight.astype(BF))
    rank = (iota((8 * CAP, n), 0) % CAP).astype(F32)
    pick = jnp.where((hit > 0.5) & (before == rank), 1.0, 0.0)
    one = pick.astype(BF)
    x = nn(one, tok_ref[...]).astype(BF)
    dy = nn(one, cot_ref[...]).astype(BF)
    p_col = jnp.sum(pick * weight, axis=1, keepdims=True)
    there = jnp.sum(pick, axis=1, keepdims=True)
    lane = iota((8 * CAP, 128), 1)
    extra = jnp.where(
        lane == 0,
        p_col,
        jnp.where(
            lane == 1, me, jnp.where(lane == 2, rank[:, :128], jnp.where(lane == 3, there, 0.0))
        ),
    ).astype(BF)
    for e in range(8):
        span = slice(e * CAP, (e + 1) * CAP)
        out_ref[e, :, 0:d] = x[span]
        out_ref[e, :, d : 2 * d] = dy[span]
        out_ref[e, :, 2 * d :] = extra[span]


def compact_kernel(in_ref, out_ref, rows_ref):
    w = in_ref.shape[2]
    slots = 8 * CAP
    for e in range(8):
        rows_ref[e * CAP : (e + 1) * CAP, :] = in_ref[e].astype(F32)
    rows = rows_ref[...].astype(BF)
    select = jnp.where(iota((8, 128), 1) == 3, 1.0, 0.0).astype(BF)
    there = nt(select, rows[:, w - 128 :])
    earlier = jnp.where(iota((slots, slots), 0) < iota((slots, slots), 1), 1.0, 0.0).astype(BF)
    place = nn(there.astype(BF), earlier)
    target = iota((RECV, slots), 0).astype(F32)
    pick = jnp.where((there[0:1] > 0.5) & (place[0:1] == target), 1.0, 0.0).astype(BF)
    out_ref[...] = nn(pick, rows).astype(BF)


def forward_kernel(count, last, *refs):
    pieces = refs[:count]
    wg_ref, wu_ref, wd_ref = refs[count : count + 3]
    metas = refs[count + 3 : -4 - last]
    dg_ref, du_ref, hp_ref, meta_ref = refs[len(refs) - 4 - last : len(refs) - last]
    d = wg_ref.shape[1]
    x = jnp.concatenate([r[:, 0:d] for r in pieces], axis=0)
    dy = jnp.concatenate([r[:, d : 2 * d] for r in pieces], axis=0)
    extra = jnp.concatenate([r[:, 2 * d :] for r in pieces], axis=0)
    select = jnp.where(iota((8, 128), 0) == iota((8, 128), 1), 1.0, 0.0).astype(BF)
    info = nt(select, extra)
    p = info[0:1]
    gate = nt(wg_ref[...], x)
    up = nt(wu_ref[...], x)
    pulled = nt(wd_ref[...], dy)
    sigma = 1.0 / (1.0 + jnp.exp(-gate))
    silu = gate * sigma
    hidden = silu * up
    router = jnp.sum(hidden.astype(BF).astype(F32) * pulled, axis=0, keepdims=True)
    d_hidden = p * pulled
    dg_ref[...] = (d_hidden * up * sigma * (1.0 + gate * (1.0 - sigma))).astype(BF)
    du_ref[...] = (d_hidden * silu).astype(BF)
    hp_ref[...] = (p * hidden).astype(BF)
    row = iota(info.shape, 0)
    meta = jnp.where(row == 0, router, info)
    meta_ref[...] = meta
    if last:
        every = jnp.concatenate([m[...] for m in metas] + [meta], axis=1)
        n = every.shape[1]
        owner = iota((256, n), 0).astype(F32)
        spread = jnp.where(every[1:2] == owner, every[0:1], 0.0)
        lanes = iota((128, n), 0).astype(F32)
        rank = jnp.where(every[2:3] == lanes, 1.0, 0.0)
        refs[-1][...] = nt(spread, rank, lax.Precision.HIGHEST)


def backward_kernel(count, groups, *refs):
    pieces_x = refs[:count]
    pieces_dy = refs[count : 2 * count]
    at = 2 * count
    dg = jnp.concatenate([r[...] for r in refs[at : at + groups]], axis=1)
    du = jnp.concatenate([r[...] for r in refs[at + groups : at + 2 * groups]], axis=1)
    hp = jnp.concatenate([r[...] for r in refs[at + 2 * groups : at + 3 * groups]], axis=1)
    og_ref, ou_ref, od_ref = refs[at + 3 * groups :]
    x = jnp.concatenate([r[...] for r in pieces_x], axis=0)
    dy = jnp.concatenate([r[...] for r in pieces_dy], axis=0)
    og_ref[0] = nn(dg, x).astype(BF)
    ou_ref[0] = nn(du, x).astype(BF)
    od_ref[0] = nn(hp, dy).astype(BF)


def collect_kernel(got_ref, ids_ref, out_ref):
    first, second, _, before = marks(ids_ref[...])
    total = got_ref[0:8, :]
    for i in range(1, got_ref.shape[0] // 8):
        total = total + got_ref[8 * i : 8 * i + 8, :]
    value = jnp.zeros(before.shape, F32)
    for j in range(CAP):
        value = value + jnp.where(before == j, total[:, j : j + 1], 0.0)
    out_ref[0:1, :] = jnp.sum(jnp.where(first, value, 0.0), axis=0, keepdims=True)
    out_ref[1:2, :] = jnp.sum(jnp.where(second, value, 0.0), axis=0, keepdims=True)


PARAMS = pltpu.CompilerParams(vmem_limit_bytes=48 * 1024 * 1024)


def move(a, axis, shift):
    n = SIZES[axis]
    return lax.ppermute(a, axis, [(i, (i + shift) % n) for i in range(n)])


def ring(s, axis):
    half = s.shape[0] // 2
    right = move(s, axis, 1)
    left = move(s, axis, 3)
    far_a = move(right[:half], axis, 1)
    far_b = move(left[half:], axis, 3)
    return jnp.concatenate([s, right, left, far_a, far_b], axis=0)


def shards(tokens, cotangent, expert_ids, gate_probs, gate_w, up_w, down_w):
    n, d = tokens.shape
    hid = gate_w.shape[1]
    w = 2 * d + 128
    ids = expert_ids.T
    send = pl.pallas_call(
        dispatch_kernel,
        out_shape=jax.ShapeDtypeStruct((8, CAP, w), BF),
        in_specs=[VMEM] * 4,
        out_specs=VMEM,
        compiler_params=PARAMS,
        name="dispatch",
    )(ids, gate_probs.T, tokens, cotangent)
    got = lax.all_to_all(send, ("y", "zl"), split_axis=0, concat_axis=0, tiled=True)
    s = pl.pallas_call(
        compact_kernel,
        out_shape=jax.ShapeDtypeStruct((RECV, w), BF),
        in_specs=[VMEM],
        out_specs=VMEM,
        scratch_shapes=[pltpu.VMEM((8 * CAP, w), F32)],
        compiler_params=PARAMS,
        name="compact",
    )(got)

    half = RECV // 2
    right = move(s, "zh", 1)
    left = move(s, "zh", 3)
    group0 = ring(s, "x")
    far = jnp.concatenate([move(right[:half], "zh", 1), move(left[half:], "zh", 3)], axis=0)
    group1 = ring(jnp.concatenate([right, left], axis=0), "x")
    group2 = ring(far, "x")
    groups = [(g, move(g, "c", 1)) for g in (group0, group1, group2)]

    weights = (gate_w[0], up_w[0], down_w[0])
    metas, dgs, dus, hps = [], [], [], []
    for i, pieces in enumerate(groups):
        last = i == len(groups) - 1
        rows = sum(q.shape[0] for q in pieces)
        outs = [jax.ShapeDtypeStruct((hid, rows), BF)] * 3
        outs.append(jax.ShapeDtypeStruct((8, rows), F32))
        if last:
            outs.append(jax.ShapeDtypeStruct((256, 128), F32))
        before = tuple(metas) if last else ()
        res = pl.pallas_call(
            functools.partial(forward_kernel, len(pieces), int(last)),
            out_shape=outs,
            in_specs=[VMEM] * (len(pieces) + 3 + len(before)),
            out_specs=[VMEM] * len(outs),
            compiler_params=PARAMS,
            name="forward",
        )(*pieces, *weights, *before)
        dgs.append(res[0])
        dus.append(res[1])
        hps.append(res[2])
        metas.append(res[3])
    router = res[4]
    returned = lax.all_to_all(router, ALL, split_axis=0, concat_axis=0, tiled=True)

    flat = [q for pieces in groups for q in pieces]
    blk = 512
    steps = d // blk
    specs = [pl.BlockSpec((q.shape[0], blk), lambda j: (0, j)) for q in flat]
    specs += [
        pl.BlockSpec((q.shape[0], blk), lambda j, off=steps: (0, j + off)) for q in flat
    ]
    for q in dgs + dus + hps:
        specs.append(pl.BlockSpec(q.shape, lambda j: (0, 0)))
    grads = pl.pallas_call(
        functools.partial(backward_kernel, len(flat), len(dgs)),
        out_shape=[jax.ShapeDtypeStruct((1, hid, d), BF)] * 3,
        grid=(steps,),
        in_specs=specs,
        out_specs=[pl.BlockSpec((1, hid, blk), lambda j: (0, 0, j))] * 3,
        compiler_params=PARAMS,
        name="backward",
    )(*flat, *flat, *dgs, *dus, *hps)

    grad_probs = pl.pallas_call(
        collect_kernel,
        out_shape=jax.ShapeDtypeStruct((2, n), F32),
        in_specs=[VMEM] * 2,
        out_specs=VMEM,
        compiler_params=PARAMS,
        name="collect",
    )(returned, ids)
    return (*grads, grad_probs.T)


def solution(mesh):
    fine = Mesh(mesh.devices.reshape([SIZES[a] for a in ALL]), ALL)
    dp, ex = ("x", "zh", "c"), ("y", "zl")
    rows = P(ALL, None)
    kept = P(ex, dp, None)
    return jax.shard_map(
        shards,
        mesh=fine,
        in_specs=(rows,) * 4 + (kept,) * 3,
        out_specs=(kept,) * 3 + (rows,),
        check_vma=False,
    )
```

time: 300 us -> 121 us (0.40)
  blocking collectives: 170 us -> 15.5 us
  matrix products: 39.3 us -> 0 us
  starting transfers between devices: 9.42 us -> 41.2 us
  waiting for transfers between devices: 51.8 us -> 23.8 us
  Pallas kernels: 0 us -> 22.9 us
  between operations: 15.4 us -> 1.02 us
  local copies, waits for them, and re-layouts: 8.39 us -> 15.3 us
    unnamed x2 -> x0, blocking collectives: 149 us -> none
    all_gather x2 -> x0, waiting for transfers between devices: 48.7 us -> none  [the longest x1 48.7 us: shards(): piece_dy = lax.all_gather(rows_dy, 'dp', axis=0, tiled=True)]
    dot_general x10 -> x0, matrix products: 39.3 us -> none  [the longest x3 17.9 us: contract_rows(): lax.dot_general(left, right, (((0,), (0,)), ((), ())), preferred_element_...]
    ppermute x0 -> x19, starting transfers between devices: none -> 35.6 us  [move(): return lax.ppermute(a, axis, [(i, (i + shift) % n) for i in range(n)])]
    ppermute x0 -> x19, waiting for transfers between devices: none -> 23.8 us  [move(): return lax.ppermute(a, axis, [(i, (i + shift) % n) for i in range(n)])]
    pallas_call x0 -> x7, Pallas kernels: none -> 22.9 us  [the longest x3 12.4 us: shards(): pl.pallas_call(functools.partial(forward_kernel, len(pieces), int(last)),...]
    unnamed x16 -> x64, local copies, waits for them, and re-layouts: 3.5 us -> 15.1 us
    all_to_all x2 -> x1, blocking collectives: 20.9 us -> 15.5 us  [shards(): lax.all_to_all(send, ('y', 'zl'), split_axis=0, concat_axis=0, tiled=True)]
  transfers between devices with their start and end apart: 4 -> 20, of which waited for: 2 -> 4; matrix products, arithmetic and copies ran while one was open for 11% -> 0% of each run, Pallas kernels for 0% -> 14%
where the time goes in v1:
time: 121 us; the launch traced here: 120 us
  starting transfers between devices  41.2 us (34%)
  waiting for transfers between devices  23.8 us (20%)
  Pallas kernels  22.9 us (19%)
  blocking collectives  15.5 us (13%)
  local copies, waits for them, and re-layouts  15.3 us (13%)
    ppermute x19, starting transfers between devices, move(): return lax.ppermute(a, axis, [(i, (i + shift) % n) for i in range(n)])  35.6 us
    ppermute x19, waiting for transfers between devices, move(): return lax.ppermute(a, axis, [(i, (i + shift) % n) for i in range(n)])  23.8 us
    all_to_all x1, blocking collectives, shards(): lax.all_to_all(send, ('y', 'zl'), split_axis=0, concat_axis=0, tiled=True)  15.5 us
    unnamed x64, local copies, waits for them, and re-layouts  15.1 us
    pallas_call x3, Pallas kernels, shards(): pl.pallas_call(functools.partial(forward_kernel, len(pieces), int(last)),...  12.4 us
    pallas_call x1, Pallas kernels, shards(): pl.pallas_call(functools.partial(backward_kernel, len(flat), len(dgs)), o...  8.71 us
    all_to_all x1, starting transfers between devices, shards(): lax.all_to_all(router, ALL, split_axis=0, concat_axis=0, tiled=True)  5.59 us
  transfers between devices with their start and end apart: 20, of which 4 were waited for; matrix products, arithmetic and copies ran while one was open for 0% of the time, Pallas kernels for 14%

profile of v1, /device:TPU:1, one launch (start us, length us, event | category | flops | bytes accessed | tf_op | source)
XLA Modules:
  0.0 119.7 jit_solution(10137535740831918693)
XLA Ops:
  0.6 1.2 %copy-done.5 = bf16[128,4096]{1,0:T(8,128)(2,1)S(1)} copy-done((bf16[128,4096]{1,0:T(8,128)(2,1)S(1)}, bf16[128,4096]{1,0:T(8,128)(2,1)}, u32[]{:S(2)}) %copy-start.5) | copy-done | bytes 1048600
  1.9 1.2 %copy-done.6 = bf16[128,4096]{1,0:T(8,128)(2,1)S(1)} copy-done((bf16[128,4096]{1,0:T(8,128)(2,1)S(1)}, bf16[128,4096]{1,0:T(8,128)(2,1)}, u32[]{:S(2)}) %copy-start.6) | copy-done | bytes 1048600
  3.1 0.7 copy-done.21
  3.8 0.7 copy-done.23
  4.4 0.6 dispatch.1
  5.1 15.5 %all_to_all.16.in_ref = bf16[8,4,8320]{2,1,0:T(4,128)(2,1)S(1)} all-to-all(bf16[8,4,8320]{2,1,0:T(4,128)(2,1)S(1)} %dispatch.1), channel_id=1, replica_groups=mesh['x'=4,'zh'=4,'c'=2,'y'=4,'zl'=2] {'y','zl'}, dimensions={0} | all-to-all | bytes 1064960 | tf_op jit(solution)/shard_map/all_to_all | solution.py:187
  20.5 0.5 compact.1
  21.0 5.2 %collective-permute-start.6 = (bf16[16,8320]{1,0:T(8,128)(2,1)S(1)}, bf16[16,8320]{1,0:T(8,128)(2,1)S(1)}, u32[]{:S(2)}, u32[]{:S(2)}) collective-permute-start(bf16[16,8320]{1,0:T(8,128)(2,1)S(1)} %compact.1), channel_id=1, source_target_pairs={{0,48},{16,0},{32,16},{48,32},{1,49},{17,1},{33,17},{49,33},{2,50}... | collective-permute-start | bytes 798728 | tf_op jit(solution)/shard_map/ppermute | solution.py:162
  26.2 0.0 collective-permute-start.5
  26.2 2.5 %collective-permute-start.1 = (bf16[16,8320]{1,0:T(8,128)(2,1)S(1)}, bf16[16,8320]{1,0:T(8,128)(2,1)S(1)}, u32[]{:S(2)}, u32[]{:S(2)}) collective-permute-start(bf16[16,8320]{1,0:T(8,128)(2,1)S(1)} %compact.1), channel_id=1, source_target_pairs={{0,192},{64,0},{128,64},{192,128},{1,193},{65,1},{129,65},{193,129... | collective-permute-start | bytes 798728 | tf_op jit(solution)/shard_map/ppermute | solution.py:162
  28.7 0.0 collective-permute-start
  28.7 10.3 %collective-permute-done.5 = bf16[16,8320]{1,0:T(8,128)(2,1)S(1)} collective-permute-done((bf16[16,8320]{1,0:T(8,128)(2,1)S(1)}, bf16[16,8320]{1,0:T(8,128)(2,1)S(1)}, u32[]{:S(2)}, u32[]{:S(2)}) %collective-permute-start.5) | collective-permute-done | bytes 266272 | tf_op jit(solution)/shard_map/ppermute | solution.py:162
  39.0 0.0 collective-permute-done.6
  39.0 2.5 %collective-permute-start.8 = (bf16[32,8320]{1,0:T(8,128)(2,1)S(1)}, bf16[32,8320]{1,0:T(8,128)(2,1)S(1)}, u32[]{:S(2)}, u32[]{:S(2)}) collective-permute-start(bf16[32,8320]{1,0:T(8,128)(2,1)S(1)} %get-tuple-element.34), channel_id=1, source_target_pairs={{0,192},{64,0},{128,64},{192,128},{1,193},{65,1},{129,65},{193,129... | collective-permute-start | bytes 1597448 | tf_op jit(solution)/shard_map/ppermute | solution.py:162
  41.6 0.0 collective-permute-start.7
  41.6 0.8 collective-permute-start.13
  42.4 0.0 collective-permute-done.1
  42.4 1.8 %collective-permute-start.12 = (bf16[8,8320]{1,0:T(8,128)(2,1)S(1)}, bf16[8,8320]{1,0:T(8,128)(2,1)S(1)}, u32[]{:S(2)}, u32[]{:S(2)}) collective-permute-start(bf16[8,8320]{1,0:T(8,128)(2,1)S(1)} %slice.36), channel_id=1, source_target_pairs={{0,16},{16,32},{32,48},{48,0},{1,17},{17,33},{33,49},{49,1},{2,18}... | collective-permute-start | bytes 399368 | tf_op jit(solution)/shard_map/ppermute | solution.py:162
  44.2 0.0 collective-permute-done
  44.2 2.8 %collective-permute-start.3 = (bf16[8,8320]{1,0:T(8,128)(2,1)S(1)}, bf16[8,8320]{1,0:T(8,128)(2,1)S(1)}, u32[]{:S(2)}, u32[]{:S(2)}) collective-permute-start(bf16[8,8320]{1,0:T(8,128)(2,1)S(1)} %slice.33), channel_id=1, source_target_pairs={{0,192},{64,0},{128,64},{192,128},{1,193},{65,1},{129,65},{193,129... | collective-permute-start | bytes 399368 | tf_op jit(solution)/shard_map/ppermute | solution.py:162
  47.0 1.5 %collective-permute-done.12 = bf16[8,8320]{1,0:T(8,128)(2,1)S(1)} collective-permute-done((bf16[8,8320]{1,0:T(8,128)(2,1)S(1)}, bf16[8,8320]{1,0:T(8,128)(2,1)S(1)}, u32[]{:S(2)}, u32[]{:S(2)}) %collective-permute-start.12) | collective-permute-done | bytes 133152 | tf_op jit(solution)/shard_map/ppermute | solution.py:162
  48.5 0.2 collective-permute-start.2
  48.7 0.0 collective-permute-done.13
  48.8 2.5 %collective-permute-start.15 = (bf16[16,8320]{1,0:T(8,128)(2,1)S(1)}, bf16[16,8320]{1,0:T(8,128)(2,1)S(1)}, u32[]{:S(2)}, u32[]{:S(2)}) collective-permute-start(bf16[16,8320]{1,0:T(8,128)(2,1)S(1)} %get-tuple-element.38), channel_id=1, source_target_pairs={{0,192},{64,0},{128,64},{192,128},{1,193},{65,1},{129,65},{193,129... | collective-permute-start | bytes 798728 | tf_op jit(solution)/shard_map/ppermute | solution.py:162
  51.3 4.4 %collective-permute-done.2 = bf16[8,8320]{1,0:T(8,128)(2,1)S(1)} collective-permute-done((bf16[8,8320]{1,0:T(8,128)(2,1)S(1)}, bf16[8,8320]{1,0:T(8,128)(2,1)S(1)}, u32[]{:S(2)}, u32[]{:S(2)}) %collective-permute-start.2) | collective-permute-done | bytes 133152 | tf_op jit(solution)/shard_map/ppermute | solution.py:162
  55.8 0.0 collective-permute-start.14
  55.8 0.0 collective-permute-done.3
  55.8 6.0 %collective-permute-start.4 = (bf16[64,8320]{1,0:T(8,128)(2,1)S(1)}, bf16[64,8320]{1,0:T(8,128)(2,1)S(1)}, u32[]{:S(2)}, u32[]{:S(2)}) collective-permute-start(bf16[64,8320]{1,0:T(8,128)(2,1)S(1)} %constant_dynamic-update-slice_fusion.refs_0_.refs_6_), channel_id=1, source_target_pairs={{0,8},{8,0},{1,9},{9,1},{2,10},{10,2},{3,11},{11,3},{4,12},{12,4},... | collective-permute-start | bytes 3194888 | tf_op jit(solution)/shard_map/ppermute | solution.py:162
  61.8 3.0 %collective-permute-start.17 = (bf16[8,8320]{1,0:T(8,128)(2,1)S(1)}, bf16[8,8320]{1,0:T(8,128)(2,1)S(1)}, u32[]{:S(2)}, u32[]{:S(2)}) collective-permute-start(bf16[8,8320]{1,0:T(8,128)(2,1)S(1)} %slice.39), channel_id=1, source_target_pairs={{0,192},{64,0},{128,64},{192,128},{1,193},{65,1},{129,65},{193,129... | collective-permute-start | bytes 399368 | tf_op jit(solution)/shard_map/ppermute | solution.py:162
  64.9 0.3 collective-permute-start.16
  65.3 2.7 %collective-permute-start.10 = (bf16[16,8320]{1,0:T(8,128)(2,1)S(1)}, bf16[16,8320]{1,0:T(8,128)(2,1)S(1)}, u32[]{:S(2)}, u32[]{:S(2)}) collective-permute-start(bf16[16,8320]{1,0:T(8,128)(2,1)S(1)} %slice.35), channel_id=1, source_target_pairs={{0,192},{64,0},{128,64},{192,128},{1,193},{65,1},{129,65},{193,129... | collective-permute-start | bytes 798728 | tf_op jit(solution)/shard_map/ppermute | solution.py:162
  68.0 0.0 collective-permute-done.7
  68.0 0.1 collective-permute-start.9
  68.1 0.0 copy-start.1
  68.2 0.0 copy-start
  68.2 7.5 %collective-permute-done.9 = bf16[16,8320]{1,0:T(8,128)(2,1)S(1)} collective-permute-done((bf16[16,8320]{1,0:T(8,128)(2,1)S(1)}, bf16[16,8320]{1,0:T(8,128)(2,1)S(1)}, u32[]{:S(2)}, u32[]{:S(2)}) %collective-permute-start.9) | collective-permute-done | bytes 266272 | tf_op jit(solution)/shard_map/ppermute | solution.py:162
  75.8 5.1 %collective-permute-start.11 = (bf16[128,8320]{1,0:T(8,128)(2,1)S(1)}, bf16[128,8320]{1,0:T(8,128)(2,1)S(1)}, u32[]{:S(2)}, u32[]{:S(2)}) collective-permute-start(bf16[128,8320]{1,0:T(8,128)(2,1)S(1)} %constant_dynamic-update-slice_fusion.7.refs_0_.refs_2_.refs_8_), channel_id=1, source_target_pairs={{0,8},{8,0},{1,9},{9,1},{2,10},{10,2},{3,11},{11,3},{4,12},{12,4},... | collective-permute-start | bytes 6389768 | tf_op jit(solution)/shard_map/ppermute | solution.py:162
  80.9 0.0 collective-permute-done.16
  80.9 0.1 collective-permute-start.18
  81.1 0.0 copy-start.2
  81.1 3.5 %forward.3 = (bf16[224,128]{1,0:T(8,128)(2,1)S(1)}, bf16[224,128]{1,0:T(8,128)(2,1)S(1)}, bf16[224,128]{1,0:T(8,128)(2,1)S(1)}, f32[8,128]{1,0:T(8,128)S(1)}) custom-call(bf16[64,8320]{1,0:T(8,128)(2,1)S(1)} %constant_dynamic-update-slice_fusion.refs_0_.refs_6_, bf16[64,8320]{1,0:T(8,128)(2,1)S(1)} %collective-permute-done.4.refs_1_.refs_7_, ...), custom_call_target="tpu_custom_call" | custom-call | tf_op jit(solution)/shard_map/forward/pallas_call | solution.py:217
  84.6 0.0 copy-start.9
  84.7 0.0 collective-permute-done.11.refs_1_.refs_3_.refs_9_
  84.7 1.4 %copy-done.25 = bf16[128,8320]{1,0:T(8,128)(2,1)} copy-done((bf16[128,8320]{1,0:T(8,128)(2,1)}, bf16[128,8320]{1,0:T(8,128)(2,1)S(1)}, u32[]{:S(2)}) %copy-start.25) | copy-done | bytes 2129944
  86.1 4.1 %forward.4 = (bf16[224,256]{1,0:T(8,128)(2,1)S(1)}, bf16[224,256]{1,0:T(8,128)(2,1)S(1)}, bf16[224,256]{1,0:T(8,128)(2,1)S(1)}, f32[8,256]{1,0:T(8,128)S(1)}) custom-call(bf16[128,8320]{1,0:T(8,128)(2,1)} %copy-done.24, bf16[128,8320]{1,0:T(8,128)(2,1)} %copy-done.25, bf16[224,4096]{1,0:T(8,128)(2,1)S(1)} %bitcast.11, bf16[224,4096]{1,0:T(8,128)(2,1)S(1)} %bitcast.14, ...), custom_call_target="tpu_custom_call" | custom-call | tf_op jit(solution)/shard_map/forward/pallas_call | solution.py:217
  90.2 0.0 copy-start.7
  90.3 0.0 collective-permute-done.18.refs_1_.refs_5_.refs_11_
  90.3 4.8 %forward.5 = (bf16[224,128]{1,0:T(8,128)(2,1)S(1)}, bf16[224,128]{1,0:T(8,128)(2,1)S(1)}, bf16[224,128]{1,0:T(8,128)(2,1)S(1)}, f32[8,128]{1,0:T(8,128)}, f32[256,128]{1,0:T(8,128)}) custom-call(bf16[64,8320]{1,0:T(8,128)(2,1)S(1)} %constant_dynamic-update-slice_fusion.15.refs_0_.refs_4_.refs_10_, ...), custom_call_target="tpu_custom_call" | custom-call | tf_op jit(solution)/shard_map/forward/pallas_call | solution.py:217
  95.0 0.6 copy-done.15
  95.7 0.6 copy-done.17
  96.3 0.7 copy-done.19
  96.9 5.6 %all-to-all-start.1 = ((f32[256,1,128]{2,1,0:T(1,128)}), f32[256,1,128]{2,1,0:T(1,128)S(1)}, u32[]{:S(2)}, u32[]{:S(2)}) async-start(f32[256,1,128]{2,1,0:T(1,128)} %bitcast.6), calls=%async_computation.1 | async-start | bytes 262144 | tf_op jit(solution)/shard_map/all_to_all | solution.py:230
  102.5 0.0 copy-start.4
  102.5 1.2 %copy-done.4 = bf16[64,8320]{1,0:T(8,128)(2,1)S(1)} copy-done((bf16[64,8320]{1,0:T(8,128)(2,1)S(1)}, bf16[64,8320]{1,0:T(8,128)(2,1)}, u32[]{:S(2)}) %copy-start.4) | copy-done | bytes 1064984
  103.8 0.9 copy-done.8
  104.7 0.8 copy-done.10
  105.5 0.8 copy-done.12
  106.3 0.8 copy-done.14
  107.1 0.8 copy-done.16
  107.9 0.8 copy-done.18
  108.8 0.8 copy-done.20
  109.6 8.7 %backward.1 = (bf16[1,224,4096]{2,1,0:T(8,128)(2,1)}, bf16[1,224,4096]{2,1,0:T(8,128)(2,1)}, bf16[1,224,4096]{2,1,0:T(8,128)(2,1)}) custom-call(bf16[64,8320]{1,0:T(8,128)(2,1)S(1)} %constant_dynamic-update-slice_fusion.refs_0_.refs_6_, bf16[64,8320]{1,0:T(8,128)(2,1)S(1)} %copy-done.4, bf16[128,8320]{1,0:T(8,128)(2,1)} %copy-done.24, ...), custom_call_target="tpu_custom_call" | custom-call | tf_op jit(solution)/shard_map/backward/pallas_call | solution.py:241
  118.3 0.7 copy-done.22
  119.0 0.7 collect.1
  (61 shorter events, 0.6 us)
Async XLA Ops:
  0.6 1.2 %copy-start.5 = (bf16[128,4096]{1,0:T(8,128)(2,1)S(1)}, bf16[128,4096]{1,0:T(8,128)(2,1)}, u32[]{:S(2)}) copy-start(bf16[128,4096]{1,0:T(8,128)(2,1)} %tok_ref.1) | copy-start | bytes 3145732
  1.9 1.2 %copy-start.6 = (bf16[128,4096]{1,0:T(8,128)(2,1)S(1)}, bf16[128,4096]{1,0:T(8,128)(2,1)}, u32[]{:S(2)}) copy-start(bf16[128,4096]{1,0:T(8,128)(2,1)} %cot_ref.1) | copy-start | bytes 3145732
  3.1 0.7 copy-start.21
  3.8 0.7 copy-start.23
  21.0 18.0 %collective-permute-start.6 = (bf16[16,8320]{1,0:T(8,128)(2,1)S(1)}, bf16[16,8320]{1,0:T(8,128)(2,1)S(1)}, u32[]{:S(2)}, u32[]{:S(2)}) collective-permute-start(bf16[16,8320]{1,0:T(8,128)(2,1)S(1)} %compact.1), channel_id=1, source_target_pairs={{0,48},{16,0},{32,16},{48,32},{1,49},{17,1},{33,17},{49,33},{2,50}... | collective-permute-start | bytes 798728 | tf_op jit(solution)/shard_map/ppermute | solution.py:162
  26.2 12.8 %collective-permute-start.5 = (bf16[16,8320]{1,0:T(8,128)(2,1)S(1)}, bf16[16,8320]{1,0:T(8,128)(2,1)S(1)}, u32[]{:S(2)}, u32[]{:S(2)}) collective-permute-start(bf16[16,8320]{1,0:T(8,128)(2,1)S(1)} %compact.1), channel_id=1, source_target_pairs={{0,16},{16,32},{32,48},{48,0},{1,17},{17,33},{33,49},{49,1},{2,18}... | collective-permute-start | bytes 798728 | tf_op jit(solution)/shard_map/ppermute | solution.py:162
  26.2 16.2 %collective-permute-start.1 = (bf16[16,8320]{1,0:T(8,128)(2,1)S(1)}, bf16[16,8320]{1,0:T(8,128)(2,1)S(1)}, u32[]{:S(2)}, u32[]{:S(2)}) collective-permute-start(bf16[16,8320]{1,0:T(8,128)(2,1)S(1)} %compact.1), channel_id=1, source_target_pairs={{0,192},{64,0},{128,64},{192,128},{1,193},{65,1},{129,65},{193,129... | collective-permute-start | bytes 798728 | tf_op jit(solution)/shard_map/ppermute | solution.py:162
  28.7 15.5 %collective-permute-start = (bf16[16,8320]{1,0:T(8,128)(2,1)S(1)}, bf16[16,8320]{1,0:T(8,128)(2,1)S(1)}, u32[]{:S(2)}, u32[]{:S(2)}) collective-permute-start(bf16[16,8320]{1,0:T(8,128)(2,1)S(1)} %compact.1), channel_id=1, source_target_pairs={{0,64},{64,128},{128,192},{192,0},{1,65},{65,129},{129,193},{193,1... | collective-permute-start | bytes 798728 | tf_op jit(solution)/shard_map/ppermute | solution.py:162
  39.0 26.2 %collective-permute-start.8 = (bf16[32,8320]{1,0:T(8,128)(2,1)S(1)}, bf16[32,8320]{1,0:T(8,128)(2,1)S(1)}, u32[]{:S(2)}, u32[]{:S(2)}) collective-permute-start(bf16[32,8320]{1,0:T(8,128)(2,1)S(1)} %get-tuple-element.34), channel_id=1, source_target_pairs={{0,192},{64,0},{128,64},{192,128},{1,193},{65,1},{129,65},{193,129... | collective-permute-start | bytes 1597448 | tf_op jit(solution)/shard_map/ppermute | solution.py:162
  41.6 26.4 %collective-permute-start.7 = (bf16[32,8320]{1,0:T(8,128)(2,1)S(1)}, bf16[32,8320]{1,0:T(8,128)(2,1)S(1)}, u32[]{:S(2)}, u32[]{:S(2)}) collective-permute-start(bf16[32,8320]{1,0:T(8,128)(2,1)S(1)} %get-tuple-element.34), channel_id=1, source_target_pairs={{0,64},{64,128},{128,192},{192,0},{1,65},{65,129},{129,193},{193,1... | collective-permute-start | bytes 1597448 | tf_op jit(solution)/shard_map/ppermute | solution.py:162
  41.6 7.1 %collective-permute-start.13 = (bf16[8,8320]{1,0:T(8,128)(2,1)S(1)}, bf16[8,8320]{1,0:T(8,128)(2,1)S(1)}, u32[]{:S(2)}, u32[]{:S(2)}) collective-permute-start(bf16[8,8320]{1,0:T(8,128)(2,1)S(1)} %slice.37), channel_id=1, source_target_pairs={{0,48},{16,0},{32,16},{48,32},{1,49},{17,1},{33,17},{49,33},{2,50}... | collective-permute-start | bytes 399368 | tf_op jit(solution)/shard_map/ppermute | solution.py:162
  42.4 6.1 %collective-permute-start.12 = (bf16[8,8320]{1,0:T(8,128)(2,1)S(1)}, bf16[8,8320]{1,0:T(8,128)(2,1)S(1)}, u32[]{:S(2)}, u32[]{:S(2)}) collective-permute-start(bf16[8,8320]{1,0:T(8,128)(2,1)S(1)} %slice.36), channel_id=1, source_target_pairs={{0,16},{16,32},{32,48},{48,0},{1,17},{17,33},{33,49},{49,1},{2,18}... | collective-permute-start | bytes 399368 | tf_op jit(solution)/shard_map/ppermute | solution.py:162
  44.2 11.6 %collective-permute-start.3 = (bf16[8,8320]{1,0:T(8,128)(2,1)S(1)}, bf16[8,8320]{1,0:T(8,128)(2,1)S(1)}, u32[]{:S(2)}, u32[]{:S(2)}) collective-permute-start(bf16[8,8320]{1,0:T(8,128)(2,1)S(1)} %slice.33), channel_id=1, source_target_pairs={{0,192},{64,0},{128,64},{192,128},{1,193},{65,1},{129,65},{193,129... | collective-permute-start | bytes 399368 | tf_op jit(solution)/shard_map/ppermute | solution.py:162
  48.5 7.3 %collective-permute-start.2 = (bf16[8,8320]{1,0:T(8,128)(2,1)S(1)}, bf16[8,8320]{1,0:T(8,128)(2,1)S(1)}, u32[]{:S(2)}, u32[]{:S(2)}) collective-permute-start(bf16[8,8320]{1,0:T(8,128)(2,1)S(1)} %slice.32), channel_id=1, source_target_pairs={{0,64},{64,128},{128,192},{192,0},{1,65},{65,129},{129,193},{193,1... | collective-permute-start | bytes 399368 | tf_op jit(solution)/shard_map/ppermute | solution.py:162
  48.8 13.0 %collective-permute-start.15 = (bf16[16,8320]{1,0:T(8,128)(2,1)S(1)}, bf16[16,8320]{1,0:T(8,128)(2,1)S(1)}, u32[]{:S(2)}, u32[]{:S(2)}) collective-permute-start(bf16[16,8320]{1,0:T(8,128)(2,1)S(1)} %get-tuple-element.38), channel_id=1, source_target_pairs={{0,192},{64,0},{128,64},{192,128},{1,193},{65,1},{129,65},{193,129... | collective-permute-start | bytes 798728 | tf_op jit(solution)/shard_map/ppermute | solution.py:162
  55.8 9.1 %collective-permute-start.14 = (bf16[16,8320]{1,0:T(8,128)(2,1)S(1)}, bf16[16,8320]{1,0:T(8,128)(2,1)S(1)}, u32[]{:S(2)}, u32[]{:S(2)}) collective-permute-start(bf16[16,8320]{1,0:T(8,128)(2,1)S(1)} %get-tuple-element.38), channel_id=1, source_target_pairs={{0,64},{64,128},{128,192},{192,0},{1,65},{65,129},{129,193},{193,1... | collective-permute-start | bytes 798728 | tf_op jit(solution)/shard_map/ppermute | solution.py:162
  55.8 25.2 %collective-permute-start.4 = (bf16[64,8320]{1,0:T(8,128)(2,1)S(1)}, bf16[64,8320]{1,0:T(8,128)(2,1)S(1)}, u32[]{:S(2)}, u32[]{:S(2)}) collective-permute-start(bf16[64,8320]{1,0:T(8,128)(2,1)S(1)} %constant_dynamic-update-slice_fusion.refs_0_.refs_6_), channel_id=1, source_target_pairs={{0,8},{8,0},{1,9},{9,1},{2,10},{10,2},{3,11},{11,3},{4,12},{12,4},... | collective-permute-start | bytes 3194888 | tf_op jit(solution)/shard_map/ppermute | solution.py:162
  61.8 19.1 %collective-permute-start.17 = (bf16[8,8320]{1,0:T(8,128)(2,1)S(1)}, bf16[8,8320]{1,0:T(8,128)(2,1)S(1)}, u32[]{:S(2)}, u32[]{:S(2)}) collective-permute-start(bf16[8,8320]{1,0:T(8,128)(2,1)S(1)} %slice.39), channel_id=1, source_target_pairs={{0,192},{64,0},{128,64},{192,128},{1,193},{65,1},{129,65},{193,129... | collective-permute-start | bytes 399368 | tf_op jit(solution)/shard_map/ppermute | solution.py:162
  64.9 16.0 %collective-permute-start.16 = (bf16[8,8320]{1,0:T(8,128)(2,1)S(1)}, bf16[8,8320]{1,0:T(8,128)(2,1)S(1)}, u32[]{:S(2)}, u32[]{:S(2)}) collective-permute-start(bf16[8,8320]{1,0:T(8,128)(2,1)S(1)} %slice.38), channel_id=1, source_target_pairs={{0,64},{64,128},{128,192},{192,0},{1,65},{65,129},{129,193},{193,1... | collective-permute-start | bytes 399368 | tf_op jit(solution)/shard_map/ppermute | solution.py:162
  65.3 10.5 %collective-permute-start.10 = (bf16[16,8320]{1,0:T(8,128)(2,1)S(1)}, bf16[16,8320]{1,0:T(8,128)(2,1)S(1)}, u32[]{:S(2)}, u32[]{:S(2)}) collective-permute-start(bf16[16,8320]{1,0:T(8,128)(2,1)S(1)} %slice.35), channel_id=1, source_target_pairs={{0,192},{64,0},{128,64},{192,128},{1,193},{65,1},{129,65},{193,129... | collective-permute-start | bytes 798728 | tf_op jit(solution)/shard_map/ppermute | solution.py:162
  68.0 7.7 %collective-permute-start.9 = (bf16[16,8320]{1,0:T(8,128)(2,1)S(1)}, bf16[16,8320]{1,0:T(8,128)(2,1)S(1)}, u32[]{:S(2)}, u32[]{:S(2)}) collective-permute-start(bf16[16,8320]{1,0:T(8,128)(2,1)S(1)} %slice.34), channel_id=1, source_target_pairs={{0,64},{64,128},{128,192},{192,0},{1,65},{65,129},{129,193},{193,1... | collective-permute-start | bytes 798728 | tf_op jit(solution)/shard_map/ppermute | solution.py:162
  68.1 12.9 %copy-start.1 = (bf16[1,224,4096]{2,1,0:T(8,128)(2,1)S(1)}, bf16[1,224,4096]{2,1,0:T(8,128)(2,1)}, u32[]{:S(2)}) copy-start(bf16[1,224,4096]{2,1,0:T(8,128)(2,1)} %param.12) | copy-start | bytes 5505028
  68.2 12.9 %copy-start = (bf16[1,224,4096]{2,1,0:T(8,128)(2,1)S(1)}, bf16[1,224,4096]{2,1,0:T(8,128)(2,1)}, u32[]{:S(2)}) copy-start(bf16[1,224,4096]{2,1,0:T(8,128)(2,1)} %param.11) | copy-start | bytes 5505028
  75.8 8.9 %copy-start.24 = (bf16[128,8320]{1,0:T(8,128)(2,1)}, bf16[128,8320]{1,0:T(8,128)(2,1)S(1)}, u32[]{:S(2)}) copy-start(bf16[128,8320]{1,0:T(8,128)(2,1)S(1)} %constant_dynamic-update-slice_fusion.7.refs_0_.refs_2_.refs_8_) | copy-start | bytes 6389764
  75.8 8.9 %collective-permute-start.11 = (bf16[128,8320]{1,0:T(8,128)(2,1)S(1)}, bf16[128,8320]{1,0:T(8,128)(2,1)S(1)}, u32[]{:S(2)}, u32[]{:S(2)}) collective-permute-start(bf16[128,8320]{1,0:T(8,128)(2,1)S(1)} %constant_dynamic-update-slice_fusion.7.refs_0_.refs_2_.refs_8_), channel_id=1, source_target_pairs={{0,8},{8,0},{1,9},{9,1},{2,10},{10,2},{3,11},{11,3},{4,12},{12,4},... | collective-permute-start | bytes 6389768 | tf_op jit(solution)/shard_map/ppermute | solution.py:162
  80.9 9.3 %collective-permute-start.18 = (bf16[64,8320]{1,0:T(8,128)(2,1)S(1)}, bf16[64,8320]{1,0:T(8,128)(2,1)S(1)}, u32[]{:S(2)}, u32[]{:S(2)}) collective-permute-start(bf16[64,8320]{1,0:T(8,128)(2,1)S(1)} %constant_dynamic-update-slice_fusion.15.refs_0_.refs_4_.refs_10_), channel_id=1, source_target_pairs={{0,8},{8,0},{1,9},{9,1},{2,10},{10,2},{3,11},{11,3},{4,12},{12,4},... | collective-permute-start | bytes 3194888 | tf_op jit(solution)/shard_map/ppermute | solution.py:162
  81.0 3.6 %copy-start.3 = (bf16[64,8320]{1,0:T(8,128)(2,1)}, bf16[64,8320]{1,0:T(8,128)(2,1)S(1)}, u32[]{:S(2)}) copy-start(bf16[64,8320]{1,0:T(8,128)(2,1)S(1)} %collective-permute-done.4.refs_1_.refs_7_) | copy-start | bytes 3194884
  81.1 5.0 %copy-start.2 = (bf16[1,224,4096]{2,1,0:T(8,128)(2,1)S(1)}, bf16[1,224,4096]{2,1,0:T(8,128)(2,1)}, u32[]{:S(2)}) copy-start(bf16[1,224,4096]{2,1,0:T(8,128)(2,1)} %param.13) | copy-start | bytes 5505028
  84.6 5.6 %copy-start.9 = (bf16[224,128]{1,0:T(8,128)(2,1)}, bf16[224,128]{1,0:T(8,128)(2,1)S(1)}, u32[]{:S(2)}) copy-start(bf16[224,128]{1,0:T(8,128)(2,1)S(1)} %get-tuple-element.19.refs_12_) | copy-start | bytes 172036
  84.7 5.6 %copy-start.11 = (bf16[224,128]{1,0:T(8,128)(2,1)}, bf16[224,128]{1,0:T(8,128)(2,1)S(1)}, u32[]{:S(2)}) copy-start(bf16[224,128]{1,0:T(8,128)(2,1)S(1)} %get-tuple-element.24.refs_15_) | copy-start | bytes 172036
  84.7 5.6 %copy-start.13 = (bf16[224,128]{1,0:T(8,128)(2,1)}, bf16[224,128]{1,0:T(8,128)(2,1)S(1)}, u32[]{:S(2)}) copy-start(bf16[224,128]{1,0:T(8,128)(2,1)S(1)} %get-tuple-element.27.refs_18_) | copy-start | bytes 172036
  84.7 1.4 %copy-start.25 = (bf16[128,8320]{1,0:T(8,128)(2,1)}, bf16[128,8320]{1,0:T(8,128)(2,1)S(1)}, u32[]{:S(2)}) copy-start(bf16[128,8320]{1,0:T(8,128)(2,1)S(1)} %collective-permute-done.11.refs_1_.refs_3_.refs_9_) | copy-start | bytes 6389764
  90.2 4.8 %copy-start.7 = (bf16[224,256]{1,0:T(8,128)(2,1)}, bf16[224,256]{1,0:T(8,128)(2,1)S(1)}, u32[]{:S(2)}) copy-start(bf16[224,256]{1,0:T(8,128)(2,1)S(1)} %get-tuple-element.28.refs_19_) | copy-start | bytes 344068
  95.0 0.6 copy-start.15
  95.7 0.6 copy-start.17
  96.3 0.7 copy-start.19
  96.9 21.4 %all-to-all-start.1 = ((f32[256,1,128]{2,1,0:T(1,128)}), f32[256,1,128]{2,1,0:T(1,128)S(1)}, u32[]{:S(2)}, u32[]{:S(2)}) async-start(f32[256,1,128]{2,1,0:T(1,128)} %bitcast.6), calls=%async_computation.1 | async-start | bytes 262144 | tf_op jit(solution)/shard_map/all_to_all | solution.py:230
  102.5 1.2 %copy-start.4 = (bf16[64,8320]{1,0:T(8,128)(2,1)S(1)}, bf16[64,8320]{1,0:T(8,128)(2,1)}, u32[]{:S(2)}) copy-start(bf16[64,8320]{1,0:T(8,128)(2,1)} %copy-done.3) | copy-start | bytes 3194884
  103.8 0.9 copy-start.8
  104.7 0.8 copy-start.10
  105.5 0.8 copy-start.12
  106.3 0.8 copy-start.14
  107.1 0.8 copy-start.16
  107.9 0.8 copy-start.18
  108.8 0.8 copy-start.20
  118.3 0.7 copy-start.22

commit v2 on v1

v2 whole, which is shorter than its diff:
```python
import functools

import jax
import jax.numpy as jnp
from jax import lax
from jax.experimental import pallas as pl
from jax.experimental.pallas import tpu as pltpu
from jax.sharding import Mesh, PartitionSpec as P

CAP = 4
RECV = 16
BF = jnp.bfloat16
F32 = jnp.float32
I32 = jnp.int32
ALL = ("x", "zh", "c", "y", "zl")
SIZES = {"x": 4, "zh": 4, "c": 2, "y": 4, "zl": 2}
VMEM = pl.BlockSpec(memory_space=pltpu.VMEM)
HBM = pl.BlockSpec(memory_space=pltpu.HBM)


def iota(shape, dim):
    return lax.broadcasted_iota(I32, shape, dim)


def nt(a, b, precision=None):
    return lax.dot_general(
        a, b, (((1,), (1,)), ((), ())), preferred_element_type=F32, precision=precision
    )


def nn(a, b):
    return lax.dot_general(a, b, (((1,), (0,)), ((), ())), preferred_element_type=F32)


def marks(ids):
    n = ids.shape[1]
    rows = iota((8, n), 0)
    first = ids[0:1, :] == rows
    second = ids[1:2, :] == rows
    hit = jnp.where(first | second, 1.0, 0.0).astype(F32)
    earlier = jnp.where(iota((n, n), 0) < iota((n, n), 1), 1.0, 0.0)
    before = nn(hit.astype(BF), earlier.astype(BF))
    return first, second, hit, before


def dispatch_kernel(
    ids_hbm, p_hbm, tok_hbm, cot_hbm, out_ref, ids_ref, p_ref, tok_ref, cot_ref, sems
):
    copies = [
        pltpu.make_async_copy(a, b, sems.at[i])
        for i, (a, b) in enumerate(
            ((ids_hbm, ids_ref), (p_hbm, p_ref), (tok_hbm, tok_ref), (cot_hbm, cot_ref))
        )
    ]
    for c in copies:
        c.start()
    d = tok_ref.shape[1]
    n = tok_ref.shape[0]
    copies[0].wait()
    copies[1].wait()
    me = lax.axis_index(ALL).astype(F32)
    first, _, hit, before = marks(ids_ref[...])
    p = p_ref[...].astype(F32)
    weight = jnp.where(first, p[0:1, :], p[1:2, :])
    spread = jnp.where(iota((8 * CAP, 8), 0) // CAP == iota((8 * CAP, 8), 1), 1.0, 0.0)
    spread = spread.astype(BF)
    hit = nn(spread, hit.astype(BF))
    before = nn(spread, before.astype(BF))
    weight = nn(spread, weight.astype(BF))
    rank = (iota((8 * CAP, n), 0) % CAP).astype(F32)
    pick = jnp.where((hit > 0.5) & (before == rank), 1.0, 0.0)
    one = pick.astype(BF)
    copies[2].wait()
    x = nn(one, tok_ref[...]).astype(BF)
    copies[3].wait()
    dy = nn(one, cot_ref[...]).astype(BF)
    p_col = jnp.sum(pick * weight, axis=1, keepdims=True)
    there = jnp.sum(pick, axis=1, keepdims=True)
    lane = iota((8 * CAP, 128), 1)
    extra = jnp.where(
        lane == 0,
        p_col,
        jnp.where(
            lane == 1, me, jnp.where(lane == 2, rank[:, :128], jnp.where(lane == 3, there, 0.0))
        ),
    ).astype(BF)
    for e in range(8):
        span = slice(e * CAP, (e + 1) * CAP)
        out_ref[e, :, 0:d] = x[span]
        out_ref[e, :, d : 2 * d] = dy[span]
        out_ref[e, :, 2 * d :] = extra[span]


def compact_kernel(in_ref, out_ref, rows_ref):
    w = in_ref.shape[2]
    slots = 8 * CAP
    for e in range(8):
        rows_ref[e * CAP : (e + 1) * CAP, :] = in_ref[e].astype(F32)
    rows = rows_ref[...].astype(BF)
    select = jnp.where(iota((8, 128), 1) == 3, 1.0, 0.0).astype(BF)
    there = nt(select, rows[:, w - 128 :])
    earlier = jnp.where(iota((slots, slots), 0) < iota((slots, slots), 1), 1.0, 0.0).astype(BF)
    place = nn(there.astype(BF), earlier)
    target = iota((RECV, slots), 0).astype(F32)
    pick = jnp.where((there[0:1] > 0.5) & (place[0:1] == target), 1.0, 0.0).astype(BF)
    out_ref[...] = nn(pick, rows).astype(BF)


def forward_kernel(spans, last, *refs):
    count = len(spans)
    *refs, dg_buf, du_buf, hp_buf, sems = refs
    pieces = [r.at[lo:hi] for r, (lo, hi) in zip(refs[:count], spans)]
    wg_ref, wu_ref, wd_ref = refs[count : count + 3]
    metas = refs[count + 3 : -5 - last]
    rows_ref, dg_ref, du_ref, hp_ref, meta_ref = refs[len(refs) - 5 - last : len(refs) - last]
    d = wg_ref.shape[1]
    copies = []
    at = 0
    for i, (lo, hi) in enumerate(spans):
        copies.append(
            pltpu.make_async_copy(pieces[i], rows_ref.at[at : at + hi - lo], sems.at[3 + i])
        )
        copies[-1].start()
        at += hi - lo
    x = jnp.concatenate([r[:, 0:d] for r in pieces], axis=0)
    dy = jnp.concatenate([r[:, d : 2 * d] for r in pieces], axis=0)
    extra = jnp.concatenate([r[:, 2 * d :] for r in pieces], axis=0)
    select = jnp.where(iota((8, 128), 0) == iota((8, 128), 1), 1.0, 0.0).astype(BF)
    info = nt(select, extra)
    p = info[0:1]
    gate = nt(wg_ref[...], x)
    up = nt(wu_ref[...], x)
    pulled = nt(wd_ref[...], dy)
    sigma = 1.0 / (1.0 + jnp.exp(-gate))
    silu = gate * sigma
    hidden = silu * up
    router = jnp.sum(hidden.astype(BF).astype(F32) * pulled, axis=0, keepdims=True)
    d_hidden = p * pulled
    dg_buf[...] = (d_hidden * up * sigma * (1.0 + gate * (1.0 - sigma))).astype(BF)
    du_buf[...] = (d_hidden * silu).astype(BF)
    hp_buf[...] = (p * hidden).astype(BF)
    for i, (a, b) in enumerate(((dg_buf, dg_ref), (du_buf, du_ref), (hp_buf, hp_ref))):
        copies.append(pltpu.make_async_copy(a, b, sems.at[i]))
        copies[-1].start()
    row = iota(info.shape, 0)
    meta = jnp.where(row == 0, router, info)
    meta_ref[...] = meta
    if last:
        every = jnp.concatenate([m[...] for m in metas] + [meta], axis=1)
        n = every.shape[1]
        owner = iota((256, n), 0).astype(F32)
        own = jnp.where(every[1:2] == owner, 1.0, 0.0).astype(BF)
        rest = every[0:1]
        parts = []
        for _ in range(3):
            top = rest.astype(BF)
            parts.append(top.astype(F32))
            rest = rest - parts[-1]
        place = iota((32, n), 0)
        value = jnp.where(place < 8, parts[0], jnp.where(place < 16, parts[1], parts[2]))
        rank = (place % 8).astype(F32)
        live = (every[2:3] == rank) & (place < 24)
        value = jnp.where(live, value, 0.0).astype(BF)
        value = jnp.concatenate([value, jnp.zeros((96, n), BF)], axis=0)
        refs[-1][...] = nt(own, value)
    for c in copies:
        c.wait()


def backward_kernel(count, groups, *refs):
    pieces = refs[:count]
    factors = refs[count : count + 3 * groups]
    outs = refs[count + 3 * groups : count + 3 * groups + 3]
    rows_ref, *fact = refs[count + 3 * groups + 3 : count + 3 * groups + 5 + groups - 1]
    bufs = refs[-6:-3]
    rows_sem, fact_sem, out_sem = refs[-3:]
    d = outs[0].shape[2]
    blk = bufs[0].shape[2]
    steps = d // blk
    loads = []
    for g in range(groups):
        for k in range(3):
            c = pltpu.make_async_copy(
                factors[k * groups + g], fact[g].at[k], fact_sem.at[g, k]
            )
            c.start()
            loads.append(c)
    fetch = []
    for j in range(steps):
        some = []
        for k in range(2):
            cols = slice(k * d + j * blk, k * d + (j + 1) * blk)
            at = 0
            for i, r in enumerate(pieces):
                c = pltpu.make_async_copy(
                    r.at[:, cols],
                    rows_ref.at[at : at + r.shape[0], cols],
                    rows_sem.at[j, k * count + i],
                )
                c.start()
                some.append(c)
                at += r.shape[0]
        fetch.append(some)
    for c in loads:
        c.wait()
    hid = fact[0].shape[1]
    both = jnp.concatenate(
        [jnp.concatenate([f[k] for f in fact], axis=1) for k in range(2)], axis=0
    )
    hp = jnp.concatenate([f[2] for f in fact], axis=1)
    flying = {}
    for j in range(steps):
        slot = j % 2
        here = slice(j * blk, (j + 1) * blk)
        there = slice(d + j * blk, d + (j + 1) * blk)
        for c in fetch[j]:
            c.wait()
        two = nn(both, rows_ref[:, here]).astype(BF)
        one = nn(hp, rows_ref[:, there]).astype(BF)
        for k, value in enumerate((two[:hid], two[hid:], one)):
            if j >= 2:
                flying[k, slot].wait()
            bufs[k][slot] = value
            flying[k, slot] = pltpu.make_async_copy(
                bufs[k].at[slot], outs[k].at[0, :, here], out_sem.at[k, slot]
            )
            flying[k, slot].start()
    for c in flying.values():
        c.wait()


def collect_kernel(got_ref, ids_ref, out_ref):
    first, second, _, before = marks(ids_ref[...])
    total = got_ref[0:8, :]
    for i in range(1, got_ref.shape[0] // 8):
        total = total + got_ref[8 * i : 8 * i + 8, :]
    value = jnp.zeros(before.shape, F32)
    for j in range(CAP):
        sums = total[:, j : j + 1] + total[:, 8 + j : 9 + j] + total[:, 16 + j : 17 + j]
        value = value + jnp.where(before == j, sums, 0.0)
    out_ref[0:1, :] = jnp.sum(jnp.where(first, value, 0.0), axis=0, keepdims=True)
    out_ref[1:2, :] = jnp.sum(jnp.where(second, value, 0.0), axis=0, keepdims=True)


def in_hbm(*arrays):
    return [pltpu.with_memory_space_constraint(a, pltpu.HBM) for a in arrays]


def limit(mib):
    return pltpu.CompilerParams(vmem_limit_bytes=mib * 1024 * 1024)


def move(a, axis, shift):
    n = SIZES[axis]
    return lax.ppermute(a, axis, [(i, (i + shift) % n) for i in range(n)])


def gate(a, *after):
    return lax.optimization_barrier((a,) + after)[0]


def shards(tokens, cotangent, expert_ids, gate_probs, gate_w, up_w, down_w):
    n, d = tokens.shape
    hid = gate_w.shape[1]
    w = 2 * d + 128
    ids = expert_ids.T
    send = pl.pallas_call(
        dispatch_kernel,
        out_shape=jax.ShapeDtypeStruct((8, CAP, w), BF),
        in_specs=[HBM] * 4,
        out_specs=VMEM,
        scratch_shapes=[
            pltpu.VMEM((2, n), I32),
            pltpu.VMEM((2, n), BF),
            pltpu.VMEM((n, d), BF),
            pltpu.VMEM((n, d), BF),
            pltpu.SemaphoreType.DMA((4,)),
        ],
        compiler_params=limit(8),
        name="dispatch",
    )(*in_hbm(ids, gate_probs.T, tokens, cotangent))
    got = lax.all_to_all(send, ("y", "zl"), split_axis=0, concat_axis=0, tiled=True)
    s = pl.pallas_call(
        compact_kernel,
        out_shape=jax.ShapeDtypeStruct((RECV, w), BF),
        in_specs=[VMEM],
        out_specs=VMEM,
        scratch_shapes=[pltpu.VMEM((8 * CAP, w), F32)],
        compiler_params=limit(4),
        name="compact",
    )(got)

    half = RECV
    z_r = move(s, "zh", 1)
    z_l = move(s, "zh", 3)
    x_r = move(s, "x", 1)
    x_l = move(s, "x", 3)
    x_2 = move(s, "x", 2)
    row_a = jnp.concatenate([s, x_r, x_l, x_2], axis=0)
    near = gate(jnp.concatenate([z_r, z_l], axis=0), x_r, x_l, x_2)
    near_r = move(near, "x", 1)
    near_l = move(near, "x", 3)
    far = move(gate(s, z_r, z_l), "zh", 2)
    row_b = jnp.concatenate([near, near_r, near_l, far], axis=0)
    far_r = move(jnp.concatenate([near_r[:half], far], axis=0), "x", 1)
    far_l = move(jnp.concatenate([near_l[half:], far], axis=0), "x", 3)
    far_x = move(gate(x_2, far), "zh", 2)
    row_c = jnp.concatenate([far_r, far_l, far_x], axis=0)
    other_a = move(row_a, "c", 1)
    other_b = move(row_b, "c", 1)
    other_c = move(gate(row_c, other_a, other_b), "c", 1)
    flat = [row_a, other_a, row_b, other_b, row_c, other_c]

    weights = (gate_w[0], up_w[0], down_w[0])
    size = sum(q.shape[0] for q in flat) // 2
    calls = ([], [])
    at = 0
    for q in flat:
        n_q = q.shape[0]
        cut = min(max(size - at, 0), n_q)
        if cut:
            calls[0].append((q, 0, cut))
        if cut < n_q:
            calls[1].append((q, cut, n_q))
        at += n_q
    stored, metas, factors = [], [], []
    for i, pieces in enumerate(calls):
        last = i == len(calls) - 1
        outs = [pltpu.HBM((size, w), BF)] + [pltpu.HBM((hid, size), BF)] * 3
        outs.append(jax.ShapeDtypeStruct((8, size), F32))
        if last:
            outs.append(jax.ShapeDtypeStruct((256, 128), F32))
        before = tuple(metas) if last else ()
        res = pl.pallas_call(
            functools.partial(forward_kernel, [q[1:] for q in pieces], int(last)),
            out_shape=outs,
            in_specs=[VMEM] * (len(pieces) + 3 + len(before)),
            out_specs=[HBM] * 4 + [VMEM] * (len(outs) - 4),
            scratch_shapes=[pltpu.VMEM((hid, size), BF)] * 3
            + [pltpu.SemaphoreType.DMA((3 + len(pieces),))],
            compiler_params=limit(16),
            name="forward",
        )(*[q[0] for q in pieces], *weights, *before)
        stored.append(res[0])
        factors.append(res[1:4])
        metas.append(res[4])
    router = res[5]
    returned = lax.all_to_all(router, ALL, split_axis=0, concat_axis=0, tiled=True)

    blk = 512
    count = len(stored)
    grads = pl.pallas_call(
        functools.partial(backward_kernel, count, count),
        out_shape=[jax.ShapeDtypeStruct((1, hid, d), BF)] * 3,
        in_specs=[HBM] * (4 * count),
        out_specs=[HBM] * 3,
        scratch_shapes=[pltpu.VMEM((count * size, w), BF)]
        + [pltpu.VMEM((3, hid, size), BF)] * count
        + [pltpu.VMEM((2, hid, blk), BF)] * 3
        + [
            pltpu.SemaphoreType.DMA((d // blk, 2 * count)),
            pltpu.SemaphoreType.DMA((count, 3)),
            pltpu.SemaphoreType.DMA((3, 2)),
        ],
        compiler_params=limit(24),
        name="backward",
    )(*in_hbm(*stored, *[f[k] for k in range(3) for f in factors]))

    grad_probs = pl.pallas_call(
        collect_kernel,
        out_shape=jax.ShapeDtypeStruct((2, n), F32),
        in_specs=[VMEM] * 2,
        out_specs=VMEM,
        compiler_params=limit(4),
        name="collect",
    )(returned, ids)
    return (*grads, grad_probs.T)


def solution(mesh):
    fine = Mesh(mesh.devices.reshape([SIZES[a] for a in ALL]), ALL)
    dp, ex = ("x", "zh", "c"), ("y", "zl")
    rows = P(ALL, None)
    kept = P(ex, dp, None)
    return jax.shard_map(
        shards,
        mesh=fine,
        in_specs=(rows,) * 4 + (kept,) * 3,
        out_specs=(kept,) * 3 + (rows,),
        check_vma=False,
    )
```

time: 121 us -> 107 us (0.88)
  local copies, waits for them, and re-layouts: 15.3 us -> 0.32 us
  Pallas kernels: 22.9 us -> 19.7 us
  waiting for transfers between devices: 23.8 us -> 26.4 us
  starting transfers between devices: 41.2 us -> 43.8 us
    unnamed x64 -> x13, local copies, waits for them, and re-layouts: 15.1 us -> 0.24 us
    all_to_all x1, starting transfers between devices: 5.59 us -> 10.6 us  [shards(): lax.all_to_all(router, ALL, split_axis=0, concat_axis=0, tiled=True)]
    pallas_call x4 -> x3, Pallas kernels: 21.1 us -> 16.6 us  [the longest x1 9.39 us: shards(): pl.pallas_call(functools.partial(backward_kernel, count, count), out_shap...]
    all_to_all x1, waiting for transfers between devices: 0.01 us -> 3.59 us  [shards(): lax.all_to_all(router, ALL, split_axis=0, concat_axis=0, tiled=True)]
    ppermute x19 -> x14, starting transfers between devices: 35.6 us -> 33.2 us  [move(): return lax.ppermute(a, axis, [(i, (i + shift) % n) for i in range(n)])]
    pallas_call x1, Pallas kernels: 0.64 us -> 1.92 us  [shards(): pl.pallas_call(dispatch_kernel, out_shape=jax.ShapeDtypeStruct((8, CAP, w...]
    ppermute x19 -> x14, waiting for transfers between devices: 23.8 us -> 22.8 us  [move(): return lax.ppermute(a, axis, [(i, (i + shift) % n) for i in range(n)])]
  transfers between devices with their start and end apart: 20 -> 15, of which waited for: 4 -> 6; matrix products, arithmetic and copies ran while one was open for 0% -> 0% of each run, Pallas kernels for 14% -> 12%
where the time goes in v2:
time: 107 us
  starting transfers between devices  43.8 us (41%)
  waiting for transfers between devices  26.4 us (25%)
  Pallas kernels  19.7 us (18%)
  blocking collectives  15.5 us (14%)
    ppermute x14, starting transfers between devices, move(): return lax.ppermute(a, axis, [(i, (i + shift) % n) for i in range(n)])  33.2 us
    ppermute x14, waiting for transfers between devices, move(): return lax.ppermute(a, axis, [(i, (i + shift) % n) for i in range(n)])  22.8 us
    all_to_all x1, blocking collectives, shards(): lax.all_to_all(send, ('y', 'zl'), split_axis=0, concat_axis=0, tiled=True)  15.5 us
    all_to_all x1, starting transfers between devices, shards(): lax.all_to_all(router, ALL, split_axis=0, concat_axis=0, tiled=True)  10.6 us
    pallas_call x1, Pallas kernels, shards(): pl.pallas_call(functools.partial(backward_kernel, count, count), out_shap...  9.39 us
    pallas_call x2, Pallas kernels, shards(): pl.pallas_call(functools.partial(forward_kernel, [q[1:] for q in pieces],...  7.21 us
    all_to_all x1, waiting for transfers between devices, shards(): lax.all_to_all(router, ALL, split_axis=0, concat_axis=0, tiled=True)  3.59 us
  transfers between devices with their start and end apart: 15, of which 6 were waited for; matrix products, arithmetic and copies ran while one was open for 0% of the time, Pallas kernels for 12%

profile of v2, /device:TPU:1, one launch (start us, length us, event | category | flops | bytes accessed | tf_op | source)
XLA Modules:
  0.0 106.7 jit_solution(2473382797318554141)
XLA Ops:
  0.6 1.9 %dispatch.1 = bf16[8,4,8320]{2,1,0:T(4,128)(2,1)S(1)} custom-call(s32[2,128]{1,0:T(2,128)} %bitcast.17, bf16[2,128]{1,0:T(2,128)(2,1)} %bitcast.20, bf16[128,4096]{1,0:T(8,128)(2,1)} %tok_hbm.1, bf16[128,4096]{1,0:T(8,128)(2,1)} %cot_hbm.1), custom_call_target="tpu_custom_call" | custom-call | tf_op jit(solution)/shard_map/dispatch/pallas_call | solution.py:267
  2.6 15.5 %all_to_all.16.in_ref = bf16[8,4,8320]{2,1,0:T(4,128)(2,1)S(1)} all-to-all(bf16[8,4,8320]{2,1,0:T(4,128)(2,1)S(1)} %dispatch.1), channel_id=1, replica_groups=mesh['x'=4,'zh'=4,'c'=2,'y'=4,'zl'=2] {'y','zl'}, dimensions={0} | all-to-all | bytes 1064960 | tf_op jit(solution)/shard_map/all_to_all | solution.py:282
  18.0 0.5 compact.1
  18.5 5.2 %collective-permute-start.5 = (bf16[16,8320]{1,0:T(8,128)(2,1)S(1)}, bf16[16,8320]{1,0:T(8,128)(2,1)S(1)}, u32[]{:S(2)}, u32[]{:S(2)}) collective-permute-start(bf16[16,8320]{1,0:T(8,128)(2,1)S(1)} %compact.1), channel_id=1, source_target_pairs={{0,48},{16,0},{32,16},{48,32},{1,49},{17,1},{33,17},{49,33},{2,50}... | collective-permute-start | bytes 798728 | tf_op jit(solution)/shard_map/ppermute | solution.py:255
  23.7 0.0 collective-permute-start.4
  23.7 2.7 %collective-permute-start.2 = (bf16[16,8320]{1,0:T(8,128)(2,1)S(1)}, bf16[16,8320]{1,0:T(8,128)(2,1)S(1)}, u32[]{:S(2)}, u32[]{:S(2)}) collective-permute-start(bf16[16,8320]{1,0:T(8,128)(2,1)S(1)} %compact.1), channel_id=1, source_target_pairs={{0,128},{64,192},{128,0},{192,64},{1,129},{65,193},{129,1},{193,65... | collective-permute-start | bytes 798728 | tf_op jit(solution)/shard_map/ppermute | solution.py:255
  26.4 0.9 collective-permute-start.1
  27.3 0.6 collective-permute-start
  27.9 6.0 %collective-permute-done.5 = bf16[16,8320]{1,0:T(8,128)(2,1)S(1)} collective-permute-done((bf16[16,8320]{1,0:T(8,128)(2,1)S(1)}, bf16[16,8320]{1,0:T(8,128)(2,1)S(1)}, u32[]{:S(2)}, u32[]{:S(2)}) %collective-permute-start.5) | collective-permute-done | bytes 266272 | tf_op jit(solution)/shard_map/ppermute | solution.py:255
  34.0 2.5 %collective-permute-done.4 = bf16[16,8320]{1,0:T(8,128)(2,1)S(1)} collective-permute-done((bf16[16,8320]{1,0:T(8,128)(2,1)S(1)}, bf16[16,8320]{1,0:T(8,128)(2,1)S(1)}, u32[]{:S(2)}, u32[]{:S(2)}) %collective-permute-start.4) | collective-permute-done | bytes 266272 | tf_op jit(solution)/shard_map/ppermute | solution.py:255
  36.5 0.0 collective-permute-done.2
  36.5 1.2 %collective-permute-done.1 = bf16[16,8320]{1,0:T(8,128)(2,1)S(1)} collective-permute-done((bf16[16,8320]{1,0:T(8,128)(2,1)S(1)}, bf16[16,8320]{1,0:T(8,128)(2,1)S(1)}, u32[]{:S(2)}, u32[]{:S(2)}) %collective-permute-start.1) | collective-permute-done | bytes 266272 | tf_op jit(solution)/shard_map/ppermute | solution.py:255
  37.7 0.0 collective-permute-done
  37.8 3.4 %collective-permute-start.7 = (bf16[32,8320]{1,0:T(8,128)(2,1)S(1)}, bf16[32,8320]{1,0:T(8,128)(2,1)S(1)}, u32[]{:S(2)}, u32[]{:S(2)}) collective-permute-start(bf16[32,8320]{1,0:T(8,128)(2,1)S(1)} %pad_maximum_fusion.3), channel_id=1, source_target_pairs={{0,192},{64,0},{128,64},{192,128},{1,193},{65,1},{129,65},{193,129... | collective-permute-start | bytes 1597448 | tf_op jit(solution)/shard_map/ppermute | solution.py:255
  41.2 0.0 collective-permute-start.6
  41.2 3.0 %collective-permute-start.8 = (bf16[16,8320]{1,0:T(8,128)(2,1)S(1)}, bf16[16,8320]{1,0:T(8,128)(2,1)S(1)}, u32[]{:S(2)}, u32[]{:S(2)}) collective-permute-start(bf16[16,8320]{1,0:T(8,128)(2,1)S(1)} %compact.1), channel_id=1, source_target_pairs={{0,32},{16,48},{32,0},{48,16},{1,33},{17,49},{33,1},{49,17},{2,34}... | collective-permute-start | bytes 798728 | tf_op jit(solution)/shard_map/ppermute | solution.py:255
  44.1 0.1 pad_maximum_fusion.refs_0_
  44.3 2.0 %collective-permute-start.3 = (bf16[64,8320]{1,0:T(8,128)(2,1)S(1)}, bf16[64,8320]{1,0:T(8,128)(2,1)S(1)}, u32[]{:S(2)}, u32[]{:S(2)}) collective-permute-start(bf16[64,8320]{1,0:T(8,128)(2,1)S(1)} %pad_maximum_fusion.refs_0_), channel_id=1, source_target_pairs={{0,8},{8,0},{1,9},{9,1},{2,10},{10,2},{3,11},{11,3},{4,12},{12,4},... | collective-permute-start | bytes 3194888 | tf_op jit(solution)/shard_map/ppermute | solution.py:255
  46.2 5.5 %collective-permute-done.8 = bf16[16,8320]{1,0:T(8,128)(2,1)S(1)} collective-permute-done((bf16[16,8320]{1,0:T(8,128)(2,1)S(1)}, bf16[16,8320]{1,0:T(8,128)(2,1)S(1)}, u32[]{:S(2)}, u32[]{:S(2)}) %collective-permute-start.8) | collective-permute-done | bytes 266272 | tf_op jit(solution)/shard_map/ppermute | solution.py:255
  51.7 4.4 %collective-permute-start.12 = (bf16[16,8320]{1,0:T(8,128)(2,1)S(1)}, bf16[16,8320]{1,0:T(8,128)(2,1)S(1)}, u32[]{:S(2)}, u32[]{:S(2)}) collective-permute-start(bf16[16,8320]{1,0:T(8,128)(2,1)S(1)} %collective-permute-done.2), channel_id=1, source_target_pairs={{0,32},{16,48},{32,0},{48,16},{1,33},{17,49},{33,1},{49,17},{2,34}... | collective-permute-start | bytes 798728 | tf_op jit(solution)/shard_map/ppermute | solution.py:255
  56.1 0.0 collective-permute-done.7
  56.1 0.0 collective-permute-done.6
  56.2 0.0 copy-start.2
  56.2 0.1 pad_maximum_fusion.1
  56.3 2.7 %collective-permute-start.11 = (bf16[32,8320]{1,0:T(8,128)(2,1)S(1)}, bf16[32,8320]{1,0:T(8,128)(2,1)S(1)}, u32[]{:S(2)}, u32[]{:S(2)}) collective-permute-start(bf16[32,8320]{1,0:T(8,128)(2,1)S(1)} %get-tuple-element.38), channel_id=1, source_target_pairs={{0,192},{64,0},{128,64},{192,128},{1,193},{65,1},{129,65},{193,129... | collective-permute-start | bytes 1597448 | tf_op jit(solution)/shard_map/ppermute | solution.py:255
  59.0 0.0 collective-permute-start.10
  59.1 0.0 copy-start.1
  59.1 0.0 copy-start
  59.2 3.6 %collective-permute-start.9 = (bf16[112,8320]{1,0:T(8,128)(2,1)S(1)}, bf16[112,8320]{1,0:T(8,128)(2,1)S(1)}, u32[]{:S(2)}, u32[]{:S(2)}) collective-permute-start(bf16[112,8320]{1,0:T(8,128)(2,1)S(1)} %constant_dynamic-update-slice_fusion.refs_2_), channel_id=1, source_target_pairs={{0,8},{8,0},{1,9},{9,1},{2,10},{10,2},{3,11},{11,3},{4,12},{12,4},... | collective-permute-start | bytes 5591048 | tf_op jit(solution)/shard_map/ppermute | solution.py:255
  62.8 7.5 %collective-permute-done.10 = bf16[32,8320]{1,0:T(8,128)(2,1)S(1)} collective-permute-done((bf16[32,8320]{1,0:T(8,128)(2,1)S(1)}, bf16[32,8320]{1,0:T(8,128)(2,1)S(1)}, u32[]{:S(2)}, u32[]{:S(2)}) %collective-permute-start.10) | collective-permute-done | bytes 532512 | tf_op jit(solution)/shard_map/ppermute | solution.py:255
  70.3 0.0 collective-permute-done.11
  70.4 0.0 collective-permute-done.12
  70.4 0.0 collective-permute-done.3.refs_1_
  70.4 0.0 collective-permute-done.9.refs_3_.refs_0_
  70.4 4.7 %collective-permute-start.13 = (bf16[80,8320]{1,0:T(8,128)(2,1)S(1)}, bf16[80,8320]{1,0:T(8,128)(2,1)S(1)}, u32[]{:S(2)}, u32[]{:S(2)}) collective-permute-start(bf16[80,8320]{1,0:T(8,128)(2,1)S(1)} %constant_dynamic-update-slice_fusion.4.refs_1_), channel_id=1, source_target_pairs={{0,8},{8,0},{1,9},{9,1},{2,10},{10,2},{3,11},{11,3},{4,12},{12,4},... | collective-permute-start | bytes 3993608 | tf_op jit(solution)/shard_map/ppermute | solution.py:255
  75.2 0.0 copy-done.2
  75.2 0.0 copy-done.1
  75.2 0.0 copy-done
  75.2 3.5 %forward.2 = (bf16[256,8320]{1,0:T(8,128)(2,1)}, bf16[224,256]{1,0:T(8,128)(2,1)}, bf16[224,256]{1,0:T(8,128)(2,1)}, bf16[224,256]{1,0:T(8,128)(2,1)}, f32[8,256]{1,0:T(8,128)S(1)}) custom-call(bf16[64,8320]{1,0:T(8,128)(2,1)S(1)} %pad_maximum_fusion.refs_0_, bf16[64,8320]{1,0:T(8,128)(2,1)S(1)} %collective-permute-done.3.refs_1_, ...), custom_call_target="tpu_custom_call" | custom-call | tf_op jit(solution)/shard_map/forward/pallas_call | solution.py:334
  78.7 0.0 collective-permute-done.13.refs_2_
  78.7 3.7 %forward.3 = (bf16[256,8320]{1,0:T(8,128)(2,1)}, bf16[224,256]{1,0:T(8,128)(2,1)}, bf16[224,256]{1,0:T(8,128)(2,1)}, bf16[224,256]{1,0:T(8,128)(2,1)}, f32[8,256]{1,0:T(8,128)}, /*index=5*/f32[256,128]{1,0:T(8,128)}) custom-call(bf16[112,8320]{1,0:T(8,128)(2,1)S(1)} %collective-permute-done.9.refs_3_.refs_0_, ...), custom_call_target="tpu_custom_call" | custom-call | tf_op jit(solution)/shard_map/forward/pallas_call | solution.py:334
  82.4 10.6 %all-to-all-start.1 = ((f32[256,1,128]{2,1,0:T(1,128)}), f32[256,1,128]{2,1,0:T(1,128)S(1)}, u32[]{:S(2)}, u32[]{:S(2)}) async-start(f32[256,1,128]{2,1,0:T(1,128)} %bitcast.6), calls=%async_computation.1 | async-start | bytes 262144 | tf_op jit(solution)/shard_map/all_to_all | solution.py:348
  93.0 0.0 copy-start.3
  93.0 9.4 %backward.1 = (bf16[1,224,4096]{2,1,0:T(8,128)(2,1)}, bf16[1,224,4096]{2,1,0:T(8,128)(2,1)}, bf16[1,224,4096]{2,1,0:T(8,128)(2,1)}) custom-call(bf16[256,8320]{1,0:T(8,128)(2,1)} %get-tuple-element.23.refs_0_, bf16[256,8320]{1,0:T(8,128)(2,1)} %get-tuple-element.27.refs_1_, bf16[224,256]{1,0:T(8,128)(2,1)} %get-tuple-element.28.refs_2_, ...), custom_call_target="tpu_custom_call" | custom-call | tf_op jit(solution)/shard_map/backward/pallas_call | solution.py:352
  102.4 3.6 %all-to-all-done.1 = f32[256,1,128]{2,1,0:T(1,128)S(1)} async-done(((f32[256,1,128]{2,1,0:T(1,128)}), f32[256,1,128]{2,1,0:T(1,128)S(1)}, u32[]{:S(2)}, u32[]{:S(2)}) %all-to-all-start.1) | async-done | bytes 131104 | tf_op jit(solution)/shard_map/all_to_all | solution.py:348
  106.0 0.0 copy-done.3
  106.0 0.7 collect.1
  (10 shorter events, 0.3 us)
Async XLA Ops:
  18.5 15.5 %collective-permute-start.5 = (bf16[16,8320]{1,0:T(8,128)(2,1)S(1)}, bf16[16,8320]{1,0:T(8,128)(2,1)S(1)}, u32[]{:S(2)}, u32[]{:S(2)}) collective-permute-start(bf16[16,8320]{1,0:T(8,128)(2,1)S(1)} %compact.1), channel_id=1, source_target_pairs={{0,48},{16,0},{32,16},{48,32},{1,49},{17,1},{33,17},{49,33},{2,50}... | collective-permute-start | bytes 798728 | tf_op jit(solution)/shard_map/ppermute | solution.py:255
  23.7 12.8 %collective-permute-start.4 = (bf16[16,8320]{1,0:T(8,128)(2,1)S(1)}, bf16[16,8320]{1,0:T(8,128)(2,1)S(1)}, u32[]{:S(2)}, u32[]{:S(2)}) collective-permute-start(bf16[16,8320]{1,0:T(8,128)(2,1)S(1)} %compact.1), channel_id=1, source_target_pairs={{0,16},{16,32},{32,48},{48,0},{1,17},{17,33},{33,49},{49,1},{2,18}... | collective-permute-start | bytes 798728 | tf_op jit(solution)/shard_map/ppermute | solution.py:255
  23.7 12.8 %collective-permute-start.2 = (bf16[16,8320]{1,0:T(8,128)(2,1)S(1)}, bf16[16,8320]{1,0:T(8,128)(2,1)S(1)}, u32[]{:S(2)}, u32[]{:S(2)}) collective-permute-start(bf16[16,8320]{1,0:T(8,128)(2,1)S(1)} %compact.1), channel_id=1, source_target_pairs={{0,128},{64,192},{128,0},{192,64},{1,129},{65,193},{129,1},{193,65... | collective-permute-start | bytes 798728 | tf_op jit(solution)/shard_map/ppermute | solution.py:255
  26.4 11.3 %collective-permute-start.1 = (bf16[16,8320]{1,0:T(8,128)(2,1)S(1)}, bf16[16,8320]{1,0:T(8,128)(2,1)S(1)}, u32[]{:S(2)}, u32[]{:S(2)}) collective-permute-start(bf16[16,8320]{1,0:T(8,128)(2,1)S(1)} %compact.1), channel_id=1, source_target_pairs={{0,192},{64,0},{128,64},{192,128},{1,193},{65,1},{129,65},{193,129... | collective-permute-start | bytes 798728 | tf_op jit(solution)/shard_map/ppermute | solution.py:255
  27.3 10.5 %collective-permute-start = (bf16[16,8320]{1,0:T(8,128)(2,1)S(1)}, bf16[16,8320]{1,0:T(8,128)(2,1)S(1)}, u32[]{:S(2)}, u32[]{:S(2)}) collective-permute-start(bf16[16,8320]{1,0:T(8,128)(2,1)S(1)} %compact.1), channel_id=1, source_target_pairs={{0,64},{64,128},{128,192},{192,0},{1,65},{65,129},{129,193},{193,1... | collective-permute-start | bytes 798728 | tf_op jit(solution)/shard_map/ppermute | solution.py:255
  37.8 18.3 %collective-permute-start.7 = (bf16[32,8320]{1,0:T(8,128)(2,1)S(1)}, bf16[32,8320]{1,0:T(8,128)(2,1)S(1)}, u32[]{:S(2)}, u32[]{:S(2)}) collective-permute-start(bf16[32,8320]{1,0:T(8,128)(2,1)S(1)} %pad_maximum_fusion.3), channel_id=1, source_target_pairs={{0,192},{64,0},{128,64},{192,128},{1,193},{65,1},{129,65},{193,129... | collective-permute-start | bytes 1597448 | tf_op jit(solution)/shard_map/ppermute | solution.py:255
  41.2 15.0 %collective-permute-start.6 = (bf16[32,8320]{1,0:T(8,128)(2,1)S(1)}, bf16[32,8320]{1,0:T(8,128)(2,1)S(1)}, u32[]{:S(2)}, u32[]{:S(2)}) collective-permute-start(bf16[32,8320]{1,0:T(8,128)(2,1)S(1)} %pad_maximum_fusion.3), channel_id=1, source_target_pairs={{0,64},{64,128},{128,192},{192,0},{1,65},{65,129},{129,193},{193,1... | collective-permute-start | bytes 1597448 | tf_op jit(solution)/shard_map/ppermute | solution.py:255
  41.2 10.5 %collective-permute-start.8 = (bf16[16,8320]{1,0:T(8,128)(2,1)S(1)}, bf16[16,8320]{1,0:T(8,128)(2,1)S(1)}, u32[]{:S(2)}, u32[]{:S(2)}) collective-permute-start(bf16[16,8320]{1,0:T(8,128)(2,1)S(1)} %compact.1), channel_id=1, source_target_pairs={{0,32},{16,48},{32,0},{48,16},{1,33},{17,49},{33,1},{49,17},{2,34}... | collective-permute-start | bytes 798728 | tf_op jit(solution)/shard_map/ppermute | solution.py:255
  44.3 26.2 %collective-permute-start.3 = (bf16[64,8320]{1,0:T(8,128)(2,1)S(1)}, bf16[64,8320]{1,0:T(8,128)(2,1)S(1)}, u32[]{:S(2)}, u32[]{:S(2)}) collective-permute-start(bf16[64,8320]{1,0:T(8,128)(2,1)S(1)} %pad_maximum_fusion.refs_0_), channel_id=1, source_target_pairs={{0,8},{8,0},{1,9},{9,1},{2,10},{10,2},{3,11},{11,3},{4,12},{12,4},... | collective-permute-start | bytes 3194888 | tf_op jit(solution)/shard_map/ppermute | solution.py:255
  51.7 18.7 %collective-permute-start.12 = (bf16[16,8320]{1,0:T(8,128)(2,1)S(1)}, bf16[16,8320]{1,0:T(8,128)(2,1)S(1)}, u32[]{:S(2)}, u32[]{:S(2)}) collective-permute-start(bf16[16,8320]{1,0:T(8,128)(2,1)S(1)} %collective-permute-done.2), channel_id=1, source_target_pairs={{0,32},{16,48},{32,0},{48,16},{1,33},{17,49},{33,1},{49,17},{2,34}... | collective-permute-start | bytes 798728 | tf_op jit(solution)/shard_map/ppermute | solution.py:255
  56.2 19.0 %copy-start.2 = (bf16[1,224,4096]{2,1,0:T(8,128)(2,1)S(1)}, bf16[1,224,4096]{2,1,0:T(8,128)(2,1)}, u32[]{:S(2)}) copy-start(bf16[1,224,4096]{2,1,0:T(8,128)(2,1)} %param.13) | copy-start | bytes 5505028
  56.3 14.1 %collective-permute-start.11 = (bf16[32,8320]{1,0:T(8,128)(2,1)S(1)}, bf16[32,8320]{1,0:T(8,128)(2,1)S(1)}, u32[]{:S(2)}, u32[]{:S(2)}) collective-permute-start(bf16[32,8320]{1,0:T(8,128)(2,1)S(1)} %get-tuple-element.38), channel_id=1, source_target_pairs={{0,192},{64,0},{128,64},{192,128},{1,193},{65,1},{129,65},{193,129... | collective-permute-start | bytes 1597448 | tf_op jit(solution)/shard_map/ppermute | solution.py:255
  59.0 11.3 %collective-permute-start.10 = (bf16[32,8320]{1,0:T(8,128)(2,1)S(1)}, bf16[32,8320]{1,0:T(8,128)(2,1)S(1)}, u32[]{:S(2)}, u32[]{:S(2)}) collective-permute-start(bf16[32,8320]{1,0:T(8,128)(2,1)S(1)} %get-tuple-element.39), channel_id=1, source_target_pairs={{0,64},{64,128},{128,192},{192,0},{1,65},{65,129},{129,193},{193,1... | collective-permute-start | bytes 1597448 | tf_op jit(solution)/shard_map/ppermute | solution.py:255
  59.1 16.1 %copy-start.1 = (bf16[1,224,4096]{2,1,0:T(8,128)(2,1)S(1)}, bf16[1,224,4096]{2,1,0:T(8,128)(2,1)}, u32[]{:S(2)}) copy-start(bf16[1,224,4096]{2,1,0:T(8,128)(2,1)} %param.12) | copy-start | bytes 5505028
  59.1 16.0 %copy-start = (bf16[1,224,4096]{2,1,0:T(8,128)(2,1)S(1)}, bf16[1,224,4096]{2,1,0:T(8,128)(2,1)}, u32[]{:S(2)}) copy-start(bf16[1,224,4096]{2,1,0:T(8,128)(2,1)} %param.11) | copy-start | bytes 5505028
  59.2 11.3 %collective-permute-start.9 = (bf16[112,8320]{1,0:T(8,128)(2,1)S(1)}, bf16[112,8320]{1,0:T(8,128)(2,1)S(1)}, u32[]{:S(2)}, u32[]{:S(2)}) collective-permute-start(bf16[112,8320]{1,0:T(8,128)(2,1)S(1)} %constant_dynamic-update-slice_fusion.refs_2_), channel_id=1, source_target_pairs={{0,8},{8,0},{1,9},{9,1},{2,10},{10,2},{3,11},{11,3},{4,12},{12,4},... | collective-permute-start | bytes 5591048 | tf_op jit(solution)/shard_map/ppermute | solution.py:255
  70.4 8.2 %collective-permute-start.13 = (bf16[80,8320]{1,0:T(8,128)(2,1)S(1)}, bf16[80,8320]{1,0:T(8,128)(2,1)S(1)}, u32[]{:S(2)}, u32[]{:S(2)}) collective-permute-start(bf16[80,8320]{1,0:T(8,128)(2,1)S(1)} %constant_dynamic-update-slice_fusion.4.refs_1_), channel_id=1, source_target_pairs={{0,8},{8,0},{1,9},{9,1},{2,10},{10,2},{3,11},{11,3},{4,12},{12,4},... | collective-permute-start | bytes 3993608 | tf_op jit(solution)/shard_map/ppermute | solution.py:255
  82.4 23.6 %all-to-all-start.1 = ((f32[256,1,128]{2,1,0:T(1,128)}), f32[256,1,128]{2,1,0:T(1,128)S(1)}, u32[]{:S(2)}, u32[]{:S(2)}) async-start(f32[256,1,128]{2,1,0:T(1,128)} %bitcast.6), calls=%async_computation.1 | async-start | bytes 262144 | tf_op jit(solution)/shard_map/all_to_all | solution.py:348
  93.0 13.0 %copy-start.3 = (s32[128,2]{0,1:T(2,128)S(1)}, s32[128,2]{0,1:T(2,128)}, u32[]{:S(2)}) copy-start(s32[128,2]{0,1:T(2,128)} %param.9) | copy-start | bytes 3076

commit v3 on v2

--- a/solution.py
+++ b/solution.py
@@ -106,22 +106,8 @@
     out_ref[...] = nn(pick, rows).astype(BF)
 
 
-def forward_kernel(spans, last, *refs):
-    count = len(spans)
-    *refs, dg_buf, du_buf, hp_buf, sems = refs
-    pieces = [r.at[lo:hi] for r, (lo, hi) in zip(refs[:count], spans)]
-    wg_ref, wu_ref, wd_ref = refs[count : count + 3]
-    metas = refs[count + 3 : -5 - last]
-    rows_ref, dg_ref, du_ref, hp_ref, meta_ref = refs[len(refs) - 5 - last : len(refs) - last]
+def forward(pieces, wg_ref, wu_ref, wd_ref):
     d = wg_ref.shape[1]
-    copies = []
-    at = 0
-    for i, (lo, hi) in enumerate(spans):
-        copies.append(
-            pltpu.make_async_copy(pieces[i], rows_ref.at[at : at + hi - lo], sems.at[3 + i])
-        )
-        copies[-1].start()
-        at += hi - lo
     x = jnp.concatenate([r[:, 0:d] for r in pieces], axis=0)
     dy = jnp.concatenate([r[:, d : 2 * d] for r in pieces], axis=0)
     extra = jnp.concatenate([r[:, 2 * d :] for r in pieces], axis=0)
@@ -136,78 +122,125 @@
     hidden = silu * up
     router = jnp.sum(hidden.astype(BF).astype(F32) * pulled, axis=0, keepdims=True)
     d_hidden = p * pulled
-    dg_buf[...] = (d_hidden * up * sigma * (1.0 + gate * (1.0 - sigma))).astype(BF)
-    du_buf[...] = (d_hidden * silu).astype(BF)
-    hp_buf[...] = (p * hidden).astype(BF)
-    for i, (a, b) in enumerate(((dg_buf, dg_ref), (du_buf, du_ref), (hp_buf, hp_ref))):
-        copies.append(pltpu.make_async_copy(a, b, sems.at[i]))
+    dg = (d_hidden * up * sigma * (1.0 + gate * (1.0 - sigma))).astype(BF)
+    du = (d_hidden * silu).astype(BF)
+    hp = (p * hidden).astype(BF)
+    return dg, du, hp, jnp.where(iota(info.shape, 0) == 0, router, info)
+
+
+def first_kernel(spans, *refs):
+    count = len(spans)
+    pieces = [r.at[lo:hi] for r, (lo, hi) in zip(refs[:count], spans)]
+    wg_ref, wu_ref, wd_ref, meta_ref, part_ref, rows_ref, buf, sems, rows_sem = refs[count:]
+    hid, d = wg_ref.shape
+    left = pltpu.make_async_copy(
+        refs[count - 1].at[spans[-1][1] : refs[count - 1].shape[0]], rows_ref, rows_sem.at[0]
+    )
+    left.start()
+    dg, du, hp, meta_ref[...] = forward(pieces, wg_ref, wu_ref, wd_ref)
+    both = jnp.concatenate([dg, du], axis=0)
+    blk = buf.shape[3]
+    flying = {}
+    for j in range(d // blk):
+        slot = j % 2
+        here = slice(j * blk, (j + 1) * blk)
+        there = slice(d + j * blk, d + (j + 1) * blk)
+        two = nn(both, jnp.concatenate([r[:, here] for r in pieces], axis=0))
+        one = nn(hp, jnp.concatenate([r[:, there] for r in pieces], axis=0))
+        for k, value in enumerate((two[:hid], two[hid:], one)):
+            if j >= 2:
+                flying[k, slot].wait()
+            buf[slot, k] = value.astype(BF)
+            flying[k, slot] = pltpu.make_async_copy(
+                buf.at[slot, k], part_ref.at[k, :, here], sems.at[slot, k]
+            )
+            flying[k, slot].start()
+    left.wait()
+    for c in flying.values():
+        c.wait()
+
+
+def last_kernel(spans, *refs):
+    count = len(spans)
+    pieces = [r.at[lo:hi] for r, (lo, hi) in zip(refs[:count], spans)]
+    (
+        wg_ref, wu_ref, wd_ref, other_ref, rows_ref, fact_ref, router_ref, fact_buf, sems
+    ) = refs[count:]
+    copies = []
+    at = 0
+    for i, (lo, hi) in enumerate(spans):
+        if i == 0:
+            continue
+        n = hi - lo
+        copies.append(
+            pltpu.make_async_copy(pieces[i], rows_ref.at[at : at + n], sems.at[i])
+        )
         copies[-1].start()
-    row = iota(info.shape, 0)
-    meta = jnp.where(row == 0, router, info)
-    meta_ref[...] = meta
-    if last:
-        every = jnp.concatenate([m[...] for m in metas] + [meta], axis=1)
-        n = every.shape[1]
-        owner = iota((256, n), 0).astype(F32)
-        own = jnp.where(every[1:2] == owner, 1.0, 0.0).astype(BF)
-        rest = every[0:1]
-        parts = []
-        for _ in range(3):
-            top = rest.astype(BF)
-            parts.append(top.astype(F32))
-            rest = rest - parts[-1]
-        place = iota((32, n), 0)
-        value = jnp.where(place < 8, parts[0], jnp.where(place < 16, parts[1], parts[2]))
-        rank = (place % 8).astype(F32)
-        live = (every[2:3] == rank) & (place < 24)
-        value = jnp.where(live, value, 0.0).astype(BF)
-        value = jnp.concatenate([value, jnp.zeros((96, n), BF)], axis=0)
-        refs[-1][...] = nt(own, value)
+        at += n
+    *three, meta = forward(pieces, wg_ref, wu_ref, wd_ref)
+    for k, value in enumerate(three):
+        fact_buf[k] = value
+        copies.append(
+            pltpu.make_async_copy(fact_buf.at[k], fact_ref.at[k], sems.at[count + k])
+        )
+        copies[-1].start()
+    every = jnp.concatenate([other_ref[...], meta], axis=1)
+    n = every.shape[1]
+    group = jnp.floor(every[1:2] * 0.125)
+    slot = (every[1:2] - 8.0 * group) * CAP + every[2:3]
+    own = jnp.where(group == iota((32, n), 0).astype(F32), 1.0, 0.0).astype(BF)
+    rest = every[0:1]
+    parts = []
+    for _ in range(3):
+        top = rest.astype(BF)
+        parts.append(top.astype(F32))
+        rest = rest - parts[-1]
+    place = iota((128, n), 0)
+    value = jnp.where(place < 32, parts[0], jnp.where(place < 64, parts[1], parts[2]))
+    live = ((place % 32).astype(F32) == slot) & (place < 96)
+    value = jnp.where(live, value, 0.0).astype(BF)
+    moved = nt(own, value)
+    mine = (iota((8, 128), 1) % 32) // CAP == iota((8, 128), 0)
+    for i in range(32):
+        router_ref[8 * i : 8 * i + 8, :] = jnp.where(mine, moved[i : i + 1, :], 0.0)
     for c in copies:
         c.wait()
 
 
-def backward_kernel(count, groups, *refs):
-    pieces = refs[:count]
-    factors = refs[count : count + 3 * groups]
-    outs = refs[count + 3 * groups : count + 3 * groups + 3]
-    rows_ref, *fact = refs[count + 3 * groups + 3 : count + 3 * groups + 5 + groups - 1]
-    bufs = refs[-6:-3]
-    rows_sem, fact_sem, out_sem = refs[-3:]
-    d = outs[0].shape[2]
-    blk = bufs[0].shape[2]
+def backward_kernel(left_hbm, rows_hbm, fact_hbm, part_hbm, *refs):
+    outs = refs[:3]
+    rows_ref, fact_ref, part_ref, buf, fact_sem, rows_sem, part_sem, out_sem = refs[3:]
+    hid, d = part_ref.shape[1:]
+    blk = buf.shape[3]
     steps = d // blk
-    loads = []
-    for g in range(groups):
-        for k in range(3):
-            c = pltpu.make_async_copy(
-                factors[k * groups + g], fact[g].at[k], fact_sem.at[g, k]
-            )
-            c.start()
-            loads.append(c)
+    fact = pltpu.make_async_copy(fact_hbm, fact_ref, fact_sem.at[0])
+    fact.start()
     fetch = []
     for j in range(steps):
         some = []
         for k in range(2):
             cols = slice(k * d + j * blk, k * d + (j + 1) * blk)
-            at = 0
-            for i, r in enumerate(pieces):
-                c = pltpu.make_async_copy(
-                    r.at[:, cols],
-                    rows_ref.at[at : at + r.shape[0], cols],
-                    rows_sem.at[j, k * count + i],
+            cut = left_hbm.shape[0]
+            some.append(
+                pltpu.make_async_copy(
+                    left_hbm.at[:, cols], rows_ref.at[0:cut, cols], rows_sem.at[j, 2 * k]
                 )
-                c.start()
-                some.append(c)
-                at += r.shape[0]
+            )
+            some.append(
+                pltpu.make_async_copy(
+                    rows_hbm.at[:, cols], rows_ref.at[cut:, cols], rows_sem.at[j, 2 * k + 1]
+                )
+            )
+        cols = slice(j * blk, (j + 1) * blk)
+        some.append(
+            pltpu.make_async_copy(part_hbm.at[:, :, cols], part_ref.at[:, :, cols], part_sem.at[j])
+        )
+        for c in some:
+            c.start()
         fetch.append(some)
-    for c in loads:
-        c.wait()
-    hid = fact[0].shape[1]
-    both = jnp.concatenate(
-        [jnp.concatenate([f[k] for f in fact], axis=1) for k in range(2)], axis=0
-    )
-    hp = jnp.concatenate([f[2] for f in fact], axis=1)
+    fact.wait()
+    both = jnp.concatenate([fact_ref[0], fact_ref[1]], axis=0)
+    hp = fact_ref[2]
     flying = {}
     for j in range(steps):
         slot = j % 2
@@ -215,14 +248,14 @@
         there = slice(d + j * blk, d + (j + 1) * blk)
         for c in fetch[j]:
             c.wait()
-        two = nn(both, rows_ref[:, here]).astype(BF)
-        one = nn(hp, rows_ref[:, there]).astype(BF)
+        two = nn(both, rows_ref[:, here])
+        one = nn(hp, rows_ref[:, there])
         for k, value in enumerate((two[:hid], two[hid:], one)):
             if j >= 2:
                 flying[k, slot].wait()
-            bufs[k][slot] = value
+            buf[slot, k] = (value + part_ref[k, :, here].astype(F32)).astype(BF)
             flying[k, slot] = pltpu.make_async_copy(
-                bufs[k].at[slot], outs[k].at[0, :, here], out_sem.at[k, slot]
+                buf.at[slot, k], outs[k].at[0, :, here], out_sem.at[slot, k]
             )
             flying[k, slot].start()
     for c in flying.values():
@@ -236,7 +269,8 @@
         total = total + got_ref[8 * i : 8 * i + 8, :]
     value = jnp.zeros(before.shape, F32)
     for j in range(CAP):
-        sums = total[:, j : j + 1] + total[:, 8 + j : 9 + j] + total[:, 16 + j : 17 + j]
+        mine = iota(total.shape, 1) % CAP == j
+        sums = jnp.sum(jnp.where(mine, total, 0.0), axis=1, keepdims=True)
         value = value + jnp.where(before == j, sums, 0.0)
     out_ref[0:1, :] = jnp.sum(jnp.where(first, value, 0.0), axis=0, keepdims=True)
     out_ref[1:2, :] = jnp.sum(jnp.where(second, value, 0.0), axis=0, keepdims=True)
@@ -302,69 +336,80 @@
     near_l = move(near, "x", 3)
     far = move(gate(s, z_r, z_l), "zh", 2)
     row_b = jnp.concatenate([near, near_r, near_l, far], axis=0)
-    far_r = move(jnp.concatenate([near_r[:half], far], axis=0), "x", 1)
+    other_a = move(row_a, "c", 1)
+    far_r = move(jnp.concatenate([near_r[:half], gate(far, other_a)], axis=0), "x", 1)
     far_l = move(jnp.concatenate([near_l[half:], far], axis=0), "x", 3)
-    far_x = move(gate(x_2, far), "zh", 2)
-    row_c = jnp.concatenate([far_r, far_l, far_x], axis=0)
-    other_a = move(row_a, "c", 1)
+    far_x = move(gate(x_2, far, near_r, near_l), "zh", 2)
     other_b = move(row_b, "c", 1)
-    other_c = move(gate(row_c, other_a, other_b), "c", 1)
-    flat = [row_a, other_a, row_b, other_b, row_c, other_c]
+    first = [row_a, other_a, row_b, other_b]
 
     weights = (gate_w[0], up_w[0], down_w[0])
-    size = sum(q.shape[0] for q in flat) // 2
-    calls = ([], [])
-    at = 0
-    for q in flat:
-        n_q = q.shape[0]
-        cut = min(max(size - at, 0), n_q)
-        if cut:
-            calls[0].append((q, 0, cut))
-        if cut < n_q:
-            calls[1].append((q, cut, n_q))
-        at += n_q
-    stored, metas, factors = [], [], []
-    for i, pieces in enumerate(calls):
-        last = i == len(calls) - 1
-        outs = [pltpu.HBM((size, w), BF)] + [pltpu.HBM((hid, size), BF)] * 3
-        outs.append(jax.ShapeDtypeStruct((8, size), F32))
-        if last:
-            outs.append(jax.ShapeDtypeStruct((256, 128), F32))
-        before = tuple(metas) if last else ()
-        res = pl.pallas_call(
-            functools.partial(forward_kernel, [q[1:] for q in pieces], int(last)),
-            out_shape=outs,
-            in_specs=[VMEM] * (len(pieces) + 3 + len(before)),
-            out_specs=[HBM] * 4 + [VMEM] * (len(outs) - 4),
-            scratch_shapes=[pltpu.VMEM((hid, size), BF)] * 3
-            + [pltpu.SemaphoreType.DMA((3 + len(pieces),))],
-            compiler_params=limit(16),
-            name="forward",
-        )(*[q[0] for q in pieces], *weights, *before)
-        stored.append(res[0])
-        factors.append(res[1:4])
-        metas.append(res[4])
-    router = res[5]
+    size = RECV * 16
+    cut = size - row_a.shape[0] * 2 - row_b.shape[0]
+    calls = (
+        [(q, 0, q.shape[0]) for q in first[:3]] + [(other_b, 0, cut)],
+        [(other_b, cut, other_b.shape[0])],
+    )
+    blk = 1024
+    head, tail = calls
+    rest = other_b.shape[0] - cut
+    meta, part, left = pl.pallas_call(
+        functools.partial(first_kernel, [q[1:] for q in head]),
+        out_shape=[
+            jax.ShapeDtypeStruct((8, size), F32),
+            pltpu.HBM((3, hid, d), BF),
+            pltpu.HBM((rest, w), BF),
+        ],
+        in_specs=[VMEM] * (len(head) + 3),
+        out_specs=[VMEM, HBM, HBM],
+        scratch_shapes=[
+            pltpu.VMEM((2, 3, hid, blk), BF),
+            pltpu.SemaphoreType.DMA((2, 3)),
+            pltpu.SemaphoreType.DMA((1,)),
+        ],
+        compiler_params=limit(16),
+        name="first",
+    )(*[q[0] for q in head], *weights)
+
+    row_c = jnp.concatenate([gate(far_r, meta), far_l, far_x], axis=0)
+    other_c = move(row_c, "c", 1)
+    tail += [(q, 0, q.shape[0]) for q in (row_c, other_c)]
+    stored, fact, router = pl.pallas_call(
+        functools.partial(last_kernel, [q[1:] for q in tail]),
+        out_shape=[
+            pltpu.HBM((size - rest, w), BF),
+            pltpu.HBM((3, hid, size), BF),
+            jax.ShapeDtypeStruct((256, 128), F32),
+        ],
+        in_specs=[VMEM] * (len(tail) + 4),
+        out_specs=[HBM, HBM, VMEM],
+        scratch_shapes=[
+            pltpu.VMEM((3, hid, size), BF),
+            pltpu.SemaphoreType.DMA((len(tail) + 3,)),
+        ],
+        compiler_params=limit(16),
+        name="last",
+    )(*[q[0] for q in tail], *weights, meta)
     returned = lax.all_to_all(router, ALL, split_axis=0, concat_axis=0, tiled=True)
 
-    blk = 512
-    count = len(stored)
     grads = pl.pallas_call(
-        functools.partial(backward_kernel, count, count),
+        backward_kernel,
         out_shape=[jax.ShapeDtypeStruct((1, hid, d), BF)] * 3,
-        in_specs=[HBM] * (4 * count),
+        in_specs=[HBM] * 4,
         out_specs=[HBM] * 3,
-        scratch_shapes=[pltpu.VMEM((count * size, w), BF)]
-        + [pltpu.VMEM((3, hid, size), BF)] * count
-        + [pltpu.VMEM((2, hid, blk), BF)] * 3
-        + [
-            pltpu.SemaphoreType.DMA((d // blk, 2 * count)),
-            pltpu.SemaphoreType.DMA((count, 3)),
-            pltpu.SemaphoreType.DMA((3, 2)),
-        ],
-        compiler_params=limit(24),
+        scratch_shapes=[
+            pltpu.VMEM((size, w), BF),
+            pltpu.VMEM((3, hid, size), BF),
+            pltpu.VMEM((3, hid, d), BF),
+            pltpu.VMEM((2, 3, hid, blk), BF),
+            pltpu.SemaphoreType.DMA((1,)),
+            pltpu.SemaphoreType.DMA((d // blk, 4)),
+            pltpu.SemaphoreType.DMA((d // blk,)),
+            pltpu.SemaphoreType.DMA((2, 3)),
+        ],
+        compiler_params=limit(32),
         name="backward",
-    )(*in_hbm(*stored, *[f[k] for k in range(3) for f in factors]))
+    )(*in_hbm(left, stored, fact, part))
 
     grad_probs = pl.pallas_call(
         collect_kernel,

time: 107 us -> 107 us (level)
  starting transfers between devices: 43.8 us -> 40.3 us
  waiting for transfers between devices: 26.4 us -> 29.5 us
    ppermute x14, starting transfers between devices: 33.2 us -> 26.8 us  [move(): return lax.ppermute(a, axis, [(i, (i + shift) % n) for i in range(n)])]
    all_to_all x1, starting transfers between devices: 10.6 us -> 13.5 us  [shards(): lax.all_to_all(router, ALL, split_axis=0, concat_axis=0, tiled=True)]
    all_to_all x1, waiting for transfers between devices: 3.59 us -> 5.58 us  [shards(): lax.all_to_all(router, ALL, split_axis=0, concat_axis=0, tiled=True)]
    ppermute x14, waiting for transfers between devices: 22.8 us -> 24 us  [move(): return lax.ppermute(a, axis, [(i, (i + shift) % n) for i in range(n)])]
  transfers between devices with their start and end apart: 15 -> 15, of which waited for: 6 -> 7; matrix products, arithmetic and copies ran while one was open for 0% -> 0% of each run, Pallas kernels for 12% -> 13%
where the time goes in v3:
time: 107 us
  starting transfers between devices  40.3 us (38%)
  waiting for transfers between devices  29.5 us (28%)
  Pallas kernels  19.9 us (19%)
  blocking collectives  15.5 us (14%)
    ppermute x14, starting transfers between devices, move(): return lax.ppermute(a, axis, [(i, (i + shift) % n) for i in range(n)])  26.8 us
    ppermute x14, waiting for transfers between devices, move(): return lax.ppermute(a, axis, [(i, (i + shift) % n) for i in range(n)])  24 us
    all_to_all x1, blocking collectives, shards(): lax.all_to_all(send, ('y', 'zl'), split_axis=0, concat_axis=0, tiled=True)  15.5 us
    all_to_all x1, starting transfers between devices, shards(): lax.all_to_all(router, ALL, split_axis=0, concat_axis=0, tiled=True)  13.5 us
    pallas_call x1, Pallas kernels, shards(): pl.pallas_call(backward_kernel, out_shape=[jax.ShapeDtypeStruct((1, hid,...  7.38 us
    pallas_call x1, Pallas kernels, shards(): pl.pallas_call(functools.partial(first_kernel, [q[1:] for q in head]), ou...  6.08 us
    all_to_all x1, waiting for transfers between devices, shards(): lax.all_to_all(router, ALL, split_axis=0, concat_axis=0, tiled=True)  5.58 us
    pallas_call x1, Pallas kernels, shards(): pl.pallas_call(functools.partial(last_kernel, [q[1:] for q in tail]), out...  3.35 us
  transfers between devices with their start and end apart: 15, of which 7 were waited for; matrix products, arithmetic and copies ran while one was open for 0% of the time, Pallas kernels for 13%

profile of v3, /device:TPU:1, one launch (start us, length us, event | category | flops | bytes accessed | tf_op | source)
XLA Modules:
  0.0 106.6 jit_solution(5090514271640001293)
XLA Ops:
  0.6 1.9 %dispatch.1 = bf16[8,4,8320]{2,1,0:T(4,128)(2,1)S(1)} custom-call(s32[2,128]{1,0:T(2,128)} %bitcast.17, bf16[2,128]{1,0:T(2,128)(2,1)} %bitcast.20, bf16[128,4096]{1,0:T(8,128)(2,1)} %tok_hbm.1, bf16[128,4096]{1,0:T(8,128)(2,1)} %cot_hbm.1), custom_call_target="tpu_custom_call" | custom-call | tf_op jit(solution)/shard_map/dispatch/pallas_call | solution.py:301
  2.6 15.5 %all_to_all.16.in_ref = bf16[8,4,8320]{2,1,0:T(4,128)(2,1)S(1)} all-to-all(bf16[8,4,8320]{2,1,0:T(4,128)(2,1)S(1)} %dispatch.1), channel_id=1, replica_groups=mesh['x'=4,'zh'=4,'c'=2,'y'=4,'zl'=2] {'y','zl'}, dimensions={0} | all-to-all | bytes 1064960 | tf_op jit(solution)/shard_map/all_to_all | solution.py:316
  18.0 0.5 compact.1
  18.5 5.2 %collective-permute-start.5 = (bf16[16,8320]{1,0:T(8,128)(2,1)S(1)}, bf16[16,8320]{1,0:T(8,128)(2,1)S(1)}, u32[]{:S(2)}, u32[]{:S(2)}) collective-permute-start(bf16[16,8320]{1,0:T(8,128)(2,1)S(1)} %compact.1), channel_id=1, source_target_pairs={{0,48},{16,0},{32,16},{48,32},{1,49},{17,1},{33,17},{49,33},{2,50}... | collective-permute-start | bytes 798728 | tf_op jit(solution)/shard_map/ppermute | solution.py:289
  23.7 0.0 collective-permute-start.4
  23.7 2.7 %collective-permute-start.2 = (bf16[16,8320]{1,0:T(8,128)(2,1)S(1)}, bf16[16,8320]{1,0:T(8,128)(2,1)S(1)}, u32[]{:S(2)}, u32[]{:S(2)}) collective-permute-start(bf16[16,8320]{1,0:T(8,128)(2,1)S(1)} %compact.1), channel_id=1, source_target_pairs={{0,128},{64,192},{128,0},{192,64},{1,129},{65,193},{129,1},{193,65... | collective-permute-start | bytes 798728 | tf_op jit(solution)/shard_map/ppermute | solution.py:289
  26.4 0.9 collective-permute-start.1
  27.3 0.6 collective-permute-start
  27.9 6.0 %collective-permute-done.5 = bf16[16,8320]{1,0:T(8,128)(2,1)S(1)} collective-permute-done((bf16[16,8320]{1,0:T(8,128)(2,1)S(1)}, bf16[16,8320]{1,0:T(8,128)(2,1)S(1)}, u32[]{:S(2)}, u32[]{:S(2)}) %collective-permute-start.5) | collective-permute-done | bytes 266272 | tf_op jit(solution)/shard_map/ppermute | solution.py:289
  34.0 2.5 %collective-permute-done.4 = bf16[16,8320]{1,0:T(8,128)(2,1)S(1)} collective-permute-done((bf16[16,8320]{1,0:T(8,128)(2,1)S(1)}, bf16[16,8320]{1,0:T(8,128)(2,1)S(1)}, u32[]{:S(2)}, u32[]{:S(2)}) %collective-permute-start.4) | collective-permute-done | bytes 266272 | tf_op jit(solution)/shard_map/ppermute | solution.py:289
  36.5 0.0 collective-permute-done.2
  36.5 1.2 %collective-permute-done.1 = bf16[16,8320]{1,0:T(8,128)(2,1)S(1)} collective-permute-done((bf16[16,8320]{1,0:T(8,128)(2,1)S(1)}, bf16[16,8320]{1,0:T(8,128)(2,1)S(1)}, u32[]{:S(2)}, u32[]{:S(2)}) %collective-permute-start.1) | collective-permute-done | bytes 266272 | tf_op jit(solution)/shard_map/ppermute | solution.py:289
  37.7 0.0 collective-permute-done
  37.8 3.4 %collective-permute-start.7 = (bf16[32,8320]{1,0:T(8,128)(2,1)S(1)}, bf16[32,8320]{1,0:T(8,128)(2,1)S(1)}, u32[]{:S(2)}, u32[]{:S(2)}) collective-permute-start(bf16[32,8320]{1,0:T(8,128)(2,1)S(1)} %pad_maximum_fusion.1), channel_id=1, source_target_pairs={{0,192},{64,0},{128,64},{192,128},{1,193},{65,1},{129,65},{193,129... | collective-permute-start | bytes 1597448 | tf_op jit(solution)/shard_map/ppermute | solution.py:289
  41.2 0.0 collective-permute-start.6
  41.2 3.0 %collective-permute-start.8 = (bf16[16,8320]{1,0:T(8,128)(2,1)S(1)}, bf16[16,8320]{1,0:T(8,128)(2,1)S(1)}, u32[]{:S(2)}, u32[]{:S(2)}) collective-permute-start(bf16[16,8320]{1,0:T(8,128)(2,1)S(1)} %compact.1), channel_id=1, source_target_pairs={{0,32},{16,48},{32,0},{48,16},{1,33},{17,49},{33,1},{49,17},{2,34}... | collective-permute-start | bytes 798728 | tf_op jit(solution)/shard_map/ppermute | solution.py:289
  44.1 0.1 pad_maximum_fusion.refs_0_
  44.2 2.0 %collective-permute-start.3 = (bf16[64,8320]{1,0:T(8,128)(2,1)S(1)}, bf16[64,8320]{1,0:T(8,128)(2,1)S(1)}, u32[]{:S(2)}, u32[]{:S(2)}) collective-permute-start(bf16[64,8320]{1,0:T(8,128)(2,1)S(1)} %pad_maximum_fusion.refs_0_), channel_id=1, source_target_pairs={{0,8},{8,0},{1,9},{9,1},{2,10},{10,2},{3,11},{11,3},{4,12},{12,4},... | collective-permute-start | bytes 3194888 | tf_op jit(solution)/shard_map/ppermute | solution.py:289
  46.2 8.4 %collective-permute-done.6 = bf16[32,8320]{1,0:T(8,128)(2,1)S(1)} collective-permute-done((bf16[32,8320]{1,0:T(8,128)(2,1)S(1)}, bf16[32,8320]{1,0:T(8,128)(2,1)S(1)}, u32[]{:S(2)}, u32[]{:S(2)}) %collective-permute-start.6) | collective-permute-done | bytes 532512 | tf_op jit(solution)/shard_map/ppermute | solution.py:289
  54.6 0.0 copy-start.2
  54.6 0.0 collective-permute-done.7
  54.7 0.0 copy-start
  54.7 0.0 copy-start.1
  54.7 0.0 collective-permute-done.8
  54.8 2.4 %collective-permute-start.9 = (bf16[112,8320]{1,0:T(8,128)(2,1)S(1)}, bf16[112,8320]{1,0:T(8,128)(2,1)S(1)}, u32[]{:S(2)}, u32[]{:S(2)}) collective-permute-start(bf16[112,8320]{1,0:T(8,128)(2,1)S(1)} %constant_dynamic-update-slice_fusion.refs_2_), channel_id=1, source_target_pairs={{0,8},{8,0},{1,9},{9,1},{2,10},{10,2},{3,11},{11,3},{4,12},{12,4},... | collective-permute-start | bytes 5591048 | tf_op jit(solution)/shard_map/ppermute | solution.py:289
  57.2 0.0 collective-permute-done.3.refs_1_
  57.3 0.1 collective-permute-start.10
  57.3 0.1 pad_maximum_fusion.3
  57.4 2.7 %collective-permute-start.11 = (bf16[32,8320]{1,0:T(8,128)(2,1)S(1)}, bf16[32,8320]{1,0:T(8,128)(2,1)S(1)}, u32[]{:S(2)}, u32[]{:S(2)}) collective-permute-start(bf16[32,8320]{1,0:T(8,128)(2,1)S(1)} %pad_maximum_fusion.3), channel_id=1, source_target_pairs={{0,192},{64,0},{128,64},{192,128},{1,193},{65,1},{129,65},{193,129... | collective-permute-start | bytes 1597448 | tf_op jit(solution)/shard_map/ppermute | solution.py:289
  60.1 3.0 %collective-permute-start.12 = (bf16[16,8320]{1,0:T(8,128)(2,1)S(1)}, bf16[16,8320]{1,0:T(8,128)(2,1)S(1)}, u32[]{:S(2)}, u32[]{:S(2)}) collective-permute-start(bf16[16,8320]{1,0:T(8,128)(2,1)S(1)} %collective-permute-done.2), channel_id=1, source_target_pairs={{0,32},{16,48},{32,0},{48,16},{1,33},{17,49},{33,1},{49,17},{2,34}... | collective-permute-start | bytes 798728 | tf_op jit(solution)/shard_map/ppermute | solution.py:289
  63.1 0.0 collective-permute-done.9.refs_3_.refs_0_
  63.1 0.0 copy-done.2
  63.1 0.0 copy-done
  63.1 0.0 copy-done.1
  63.1 6.1 %first.1 = (f32[8,256]{1,0:T(8,128)S(1)}, bf16[3,224,4096]{2,1,0:T(8,128)(2,1)}, bf16[96,8320]{1,0:T(8,128)(2,1)}) custom-call(bf16[64,8320]{1,0:T(8,128)(2,1)S(1)} %pad_maximum_fusion.refs_0_, bf16[64,8320]{1,0:T(8,128)(2,1)S(1)} %collective-permute-done.3.refs_1_, bf16[112,8320]{1,0:T(8,128)(2,1)S(1)} %constant_dynamic-update-slice_fusion.refs_2_, ...), custom_call_target="tpu_custom_call" | custom-call | tf_op jit(solution)/shard_map/first/pallas_call | solution.py:356
  69.2 3.0 %collective-permute-done.10 = bf16[32,8320]{1,0:T(8,128)(2,1)S(1)} collective-permute-done((bf16[32,8320]{1,0:T(8,128)(2,1)S(1)}, bf16[32,8320]{1,0:T(8,128)(2,1)S(1)}, u32[]{:S(2)}, u32[]{:S(2)}) %collective-permute-start.10) | collective-permute-done | bytes 532512 | tf_op jit(solution)/shard_map/ppermute | solution.py:289
  72.3 0.0 collective-permute-done.11
  72.4 0.0 collective-permute-done.12
  72.4 0.9 collective-permute-start.13
  73.3 2.7 %collective-permute-done.13.refs_2_ = bf16[80,8320]{1,0:T(8,128)(2,1)S(1)} collective-permute-done((bf16[80,8320]{1,0:T(8,128)(2,1)S(1)}, bf16[80,8320]{1,0:T(8,128)(2,1)S(1)}, u32[]{:S(2)}, u32[]{:S(2)}) %collective-permute-start.13) | collective-permute-done | bytes 1331232 | tf_op jit(solution)/shard_map/ppermute | solution.py:289
  76.0 3.3 %last.1 = (bf16[160,8320]{1,0:T(8,128)(2,1)}, bf16[3,224,256]{2,1,0:T(8,128)(2,1)}, f32[256,128]{1,0:T(8,128)}) custom-call(bf16[112,8320]{1,0:T(8,128)(2,1)S(1)} %collective-permute-done.9.refs_3_.refs_0_, bf16[80,8320]{1,0:T(8,128)(2,1)S(1)} %constant_dynamic-update-slice_fusion.4.refs_1_, bf16[80,8320]{1,0:T(8,128)(2,1)S(1)} %collective-permute-done.13.refs_2_, ...), custom_call_target="tpu_custom_call" | custom-call | tf_op jit(solution)/shard_map/last/pallas_call | solution.py:377
  79.3 13.5 %all-to-all-start.1 = ((f32[256,1,128]{2,1,0:T(1,128)}), f32[256,1,128]{2,1,0:T(1,128)S(1)}, u32[]{:S(2)}, u32[]{:S(2)}) async-start(f32[256,1,128]{2,1,0:T(1,128)} %bitcast.6), calls=%async_computation.1 | async-start | bytes 262144 | tf_op jit(solution)/shard_map/all_to_all | solution.py:393
  92.9 0.0 copy-start.3
  92.9 7.4 %backward.1 = (bf16[1,224,4096]{2,1,0:T(8,128)(2,1)}, bf16[1,224,4096]{2,1,0:T(8,128)(2,1)}, bf16[1,224,4096]{2,1,0:T(8,128)(2,1)}) custom-call(bf16[96,8320]{1,0:T(8,128)(2,1)} %get-tuple-element.20.left_hbm, bf16[160,8320]{1,0:T(8,128)(2,1)} %get-tuple-element.25.rows_hbm, bf16[3,224,256]{2,1,0:T(8,128)(2,1)} %get-tuple-element.26.fact_hbm, ...), custom_call_target="tpu_custom_call" | custom-call | tf_op jit(solution)/shard_map/backward/pallas_call | solution.py:395
  100.3 5.6 %all-to-all-done.1 = f32[256,1,128]{2,1,0:T(1,128)S(1)} async-done(((f32[256,1,128]{2,1,0:T(1,128)}), f32[256,1,128]{2,1,0:T(1,128)S(1)}, u32[]{:S(2)}, u32[]{:S(2)}) %all-to-all-start.1) | async-done | bytes 131104 | tf_op jit(solution)/shard_map/all_to_all | solution.py:393
  105.9 0.0 copy-done.3
  105.9 0.7 collect.1
  (11 shorter events, 0.4 us)
Async XLA Ops:
  18.5 15.5 %collective-permute-start.5 = (bf16[16,8320]{1,0:T(8,128)(2,1)S(1)}, bf16[16,8320]{1,0:T(8,128)(2,1)S(1)}, u32[]{:S(2)}, u32[]{:S(2)}) collective-permute-start(bf16[16,8320]{1,0:T(8,128)(2,1)S(1)} %compact.1), channel_id=1, source_target_pairs={{0,48},{16,0},{32,16},{48,32},{1,49},{17,1},{33,17},{49,33},{2,50}... | collective-permute-start | bytes 798728 | tf_op jit(solution)/shard_map/ppermute | solution.py:289
  23.7 12.8 %collective-permute-start.4 = (bf16[16,8320]{1,0:T(8,128)(2,1)S(1)}, bf16[16,8320]{1,0:T(8,128)(2,1)S(1)}, u32[]{:S(2)}, u32[]{:S(2)}) collective-permute-start(bf16[16,8320]{1,0:T(8,128)(2,1)S(1)} %compact.1), channel_id=1, source_target_pairs={{0,16},{16,32},{32,48},{48,0},{1,17},{17,33},{33,49},{49,1},{2,18}... | collective-permute-start | bytes 798728 | tf_op jit(solution)/shard_map/ppermute | solution.py:289
  23.7 12.8 %collective-permute-start.2 = (bf16[16,8320]{1,0:T(8,128)(2,1)S(1)}, bf16[16,8320]{1,0:T(8,128)(2,1)S(1)}, u32[]{:S(2)}, u32[]{:S(2)}) collective-permute-start(bf16[16,8320]{1,0:T(8,128)(2,1)S(1)} %compact.1), channel_id=1, source_target_pairs={{0,128},{64,192},{128,0},{192,64},{1,129},{65,193},{129,1},{193,65... | collective-permute-start | bytes 798728 | tf_op jit(solution)/shard_map/ppermute | solution.py:289
  26.4 11.3 %collective-permute-start.1 = (bf16[16,8320]{1,0:T(8,128)(2,1)S(1)}, bf16[16,8320]{1,0:T(8,128)(2,1)S(1)}, u32[]{:S(2)}, u32[]{:S(2)}) collective-permute-start(bf16[16,8320]{1,0:T(8,128)(2,1)S(1)} %compact.1), channel_id=1, source_target_pairs={{0,192},{64,0},{128,64},{192,128},{1,193},{65,1},{129,65},{193,129... | collective-permute-start | bytes 798728 | tf_op jit(solution)/shard_map/ppermute | solution.py:289
  27.3 10.5 %collective-permute-start = (bf16[16,8320]{1,0:T(8,128)(2,1)S(1)}, bf16[16,8320]{1,0:T(8,128)(2,1)S(1)}, u32[]{:S(2)}, u32[]{:S(2)}) collective-permute-start(bf16[16,8320]{1,0:T(8,128)(2,1)S(1)} %compact.1), channel_id=1, source_target_pairs={{0,64},{64,128},{128,192},{192,0},{1,65},{65,129},{129,193},{193,1... | collective-permute-start | bytes 798728 | tf_op jit(solution)/shard_map/ppermute | solution.py:289
  37.8 16.9 %collective-permute-start.7 = (bf16[32,8320]{1,0:T(8,128)(2,1)S(1)}, bf16[32,8320]{1,0:T(8,128)(2,1)S(1)}, u32[]{:S(2)}, u32[]{:S(2)}) collective-permute-start(bf16[32,8320]{1,0:T(8,128)(2,1)S(1)} %pad_maximum_fusion.1), channel_id=1, source_target_pairs={{0,192},{64,0},{128,64},{192,128},{1,193},{65,1},{129,65},{193,129... | collective-permute-start | bytes 1597448 | tf_op jit(solution)/shard_map/ppermute | solution.py:289
  41.2 13.4 %collective-permute-start.6 = (bf16[32,8320]{1,0:T(8,128)(2,1)S(1)}, bf16[32,8320]{1,0:T(8,128)(2,1)S(1)}, u32[]{:S(2)}, u32[]{:S(2)}) collective-permute-start(bf16[32,8320]{1,0:T(8,128)(2,1)S(1)} %pad_maximum_fusion.1), channel_id=1, source_target_pairs={{0,64},{64,128},{128,192},{192,0},{1,65},{65,129},{129,193},{193,1... | collective-permute-start | bytes 1597448 | tf_op jit(solution)/shard_map/ppermute | solution.py:289
  41.2 13.6 %collective-permute-start.8 = (bf16[16,8320]{1,0:T(8,128)(2,1)S(1)}, bf16[16,8320]{1,0:T(8,128)(2,1)S(1)}, u32[]{:S(2)}, u32[]{:S(2)}) collective-permute-start(bf16[16,8320]{1,0:T(8,128)(2,1)S(1)} %compact.1), channel_id=1, source_target_pairs={{0,32},{16,48},{32,0},{48,16},{1,33},{17,49},{33,1},{49,17},{2,34}... | collective-permute-start | bytes 798728 | tf_op jit(solution)/shard_map/ppermute | solution.py:289
  44.2 13.0 %collective-permute-start.3 = (bf16[64,8320]{1,0:T(8,128)(2,1)S(1)}, bf16[64,8320]{1,0:T(8,128)(2,1)S(1)}, u32[]{:S(2)}, u32[]{:S(2)}) collective-permute-start(bf16[64,8320]{1,0:T(8,128)(2,1)S(1)} %pad_maximum_fusion.refs_0_), channel_id=1, source_target_pairs={{0,8},{8,0},{1,9},{9,1},{2,10},{10,2},{3,11},{11,3},{4,12},{12,4},... | collective-permute-start | bytes 3194888 | tf_op jit(solution)/shard_map/ppermute | solution.py:289
  54.6 8.5 %copy-start.2 = (bf16[1,224,4096]{2,1,0:T(8,128)(2,1)S(1)}, bf16[1,224,4096]{2,1,0:T(8,128)(2,1)}, u32[]{:S(2)}) copy-start(bf16[1,224,4096]{2,1,0:T(8,128)(2,1)} %param.13) | copy-start | bytes 5505028
  54.7 8.4 %copy-start = (bf16[1,224,4096]{2,1,0:T(8,128)(2,1)S(1)}, bf16[1,224,4096]{2,1,0:T(8,128)(2,1)}, u32[]{:S(2)}) copy-start(bf16[1,224,4096]{2,1,0:T(8,128)(2,1)} %param.11) | copy-start | bytes 5505028
  54.7 8.4 %copy-start.1 = (bf16[1,224,4096]{2,1,0:T(8,128)(2,1)S(1)}, bf16[1,224,4096]{2,1,0:T(8,128)(2,1)}, u32[]{:S(2)}) copy-start(bf16[1,224,4096]{2,1,0:T(8,128)(2,1)} %param.12) | copy-start | bytes 5505028
  54.8 8.3 %collective-permute-start.9 = (bf16[112,8320]{1,0:T(8,128)(2,1)S(1)}, bf16[112,8320]{1,0:T(8,128)(2,1)S(1)}, u32[]{:S(2)}, u32[]{:S(2)}) collective-permute-start(bf16[112,8320]{1,0:T(8,128)(2,1)S(1)} %constant_dynamic-update-slice_fusion.refs_2_), channel_id=1, source_target_pairs={{0,8},{8,0},{1,9},{9,1},{2,10},{10,2},{3,11},{11,3},{4,12},{12,4},... | collective-permute-start | bytes 5591048 | tf_op jit(solution)/shard_map/ppermute | solution.py:289
  57.3 15.0 %collective-permute-start.10 = (bf16[32,8320]{1,0:T(8,128)(2,1)S(1)}, bf16[32,8320]{1,0:T(8,128)(2,1)S(1)}, u32[]{:S(2)}, u32[]{:S(2)}) collective-permute-start(bf16[32,8320]{1,0:T(8,128)(2,1)S(1)} %pad_maximum_fusion.2), channel_id=1, source_target_pairs={{0,64},{64,128},{128,192},{192,0},{1,65},{65,129},{129,193},{193,1... | collective-permute-start | bytes 1597448 | tf_op jit(solution)/shard_map/ppermute | solution.py:289
  57.4 14.9 %collective-permute-start.11 = (bf16[32,8320]{1,0:T(8,128)(2,1)S(1)}, bf16[32,8320]{1,0:T(8,128)(2,1)S(1)}, u32[]{:S(2)}, u32[]{:S(2)}) collective-permute-start(bf16[32,8320]{1,0:T(8,128)(2,1)S(1)} %pad_maximum_fusion.3), channel_id=1, source_target_pairs={{0,192},{64,0},{128,64},{192,128},{1,193},{65,1},{129,65},{193,129... | collective-permute-start | bytes 1597448 | tf_op jit(solution)/shard_map/ppermute | solution.py:289
  60.1 12.2 %collective-permute-start.12 = (bf16[16,8320]{1,0:T(8,128)(2,1)S(1)}, bf16[16,8320]{1,0:T(8,128)(2,1)S(1)}, u32[]{:S(2)}, u32[]{:S(2)}) collective-permute-start(bf16[16,8320]{1,0:T(8,128)(2,1)S(1)} %collective-permute-done.2), channel_id=1, source_target_pairs={{0,32},{16,48},{32,0},{48,16},{1,33},{17,49},{33,1},{49,17},{2,34}... | collective-permute-start | bytes 798728 | tf_op jit(solution)/shard_map/ppermute | solution.py:289
  72.4 3.6 %collective-permute-start.13 = (bf16[80,8320]{1,0:T(8,128)(2,1)S(1)}, bf16[80,8320]{1,0:T(8,128)(2,1)S(1)}, u32[]{:S(2)}, u32[]{:S(2)}) collective-permute-start(bf16[80,8320]{1,0:T(8,128)(2,1)S(1)} %constant_dynamic-update-slice_fusion.4.refs_1_), channel_id=1, source_target_pairs={{0,8},{8,0},{1,9},{9,1},{2,10},{10,2},{3,11},{11,3},{4,12},{12,4},... | collective-permute-start | bytes 3993608 | tf_op jit(solution)/shard_map/ppermute | solution.py:289
  79.3 26.5 %all-to-all-start.1 = ((f32[256,1,128]{2,1,0:T(1,128)}), f32[256,1,128]{2,1,0:T(1,128)S(1)}, u32[]{:S(2)}, u32[]{:S(2)}) async-start(f32[256,1,128]{2,1,0:T(1,128)} %bitcast.6), calls=%async_computation.1 | async-start | bytes 262144 | tf_op jit(solution)/shard_map/all_to_all | solution.py:393
  92.9 13.0 %copy-start.3 = (s32[128,2]{0,1:T(2,128)S(1)}, s32[128,2]{0,1:T(2,128)}, u32[]{:S(2)}) copy-start(s32[128,2]{0,1:T(2,128)} %param.9) | copy-start | bytes 3076

commit v4 on v3

--- a/solution.py
+++ b/solution.py
@@ -371,9 +371,11 @@
         name="first",
     )(*[q[0] for q in head], *weights)
 
-    row_c = jnp.concatenate([gate(far_r, meta), far_l, far_x], axis=0)
+    row_c = gate(far_r, meta)
     other_c = move(row_c, "c", 1)
-    tail += [(q, 0, q.shape[0]) for q in (row_c, other_c)]
+    row_d = jnp.concatenate([far_l, far_x], axis=0)
+    other_d = move(row_d, "c", 1)
+    tail += [(q, 0, q.shape[0]) for q in (row_c, other_c, row_d, other_d)]
     stored, fact, router = pl.pallas_call(
         functools.partial(last_kernel, [q[1:] for q in tail]),
         out_shape=[

time: 107 us -> 114 us (1.065)
  starting transfers between devices: 40.3 us -> 52.8 us
  waiting for transfers between devices: 29.5 us -> 24.1 us
    ppermute x14 -> x15, starting transfers between devices: 26.8 us -> 38.1 us  [move(): return lax.ppermute(a, axis, [(i, (i + shift) % n) for i in range(n)])]
    ppermute x14 -> x15, waiting for transfers between devices: 24 us -> 18.5 us  [move(): return lax.ppermute(a, axis, [(i, (i + shift) % n) for i in range(n)])]
    all_to_all x1, starting transfers between devices: 13.5 us -> 14.8 us  [shards(): lax.all_to_all(router, ALL, split_axis=0, concat_axis=0, tiled=True)]
  transfers between devices with their start and end apart: 15 -> 16, of which waited for: 7 -> 10; matrix products, arithmetic and copies ran while one was open for 0% -> 0% of each run, Pallas kernels for 13% -> 12%
where the time goes in v4:
time: 114 us
  starting transfers between devices  52.8 us (46%)
  waiting for transfers between devices  24.1 us (21%)
  Pallas kernels  20.4 us (18%)
  blocking collectives  15.5 us (14%)
    ppermute x15, starting transfers between devices, move(): return lax.ppermute(a, axis, [(i, (i + shift) % n) for i in range(n)])  38.1 us
    ppermute x15, waiting for transfers between devices, move(): return lax.ppermute(a, axis, [(i, (i + shift) % n) for i in range(n)])  18.5 us
    all_to_all x1, blocking collectives, shards(): lax.all_to_all(send, ('y', 'zl'), split_axis=0, concat_axis=0, tiled=True)  15.5 us
    all_to_all x1, starting transfers between devices, shards(): lax.all_to_all(router, ALL, split_axis=0, concat_axis=0, tiled=True)  14.8 us
    pallas_call x1, Pallas kernels, shards(): pl.pallas_call(backward_kernel, out_shape=[jax.ShapeDtypeStruct((1, hid,...  7.38 us
    pallas_call x1, Pallas kernels, shards(): pl.pallas_call(functools.partial(first_kernel, [q[1:] for q in head]), ou...  6.07 us
    all_to_all x1, waiting for transfers between devices, shards(): lax.all_to_all(router, ALL, split_axis=0, concat_axis=0, tiled=True)  5.61 us
    pallas_call x1, Pallas kernels, shards(): pl.pallas_call(functools.partial(last_kernel, [q[1:] for q in tail]), out...  3.86 us
  transfers between devices with their start and end apart: 16, of which 10 were waited for; matrix products, arithmetic and copies ran while one was open for 0% of the time, Pallas kernels for 12%

profile of v4, /device:TPU:1, one launch (start us, length us, event | category | flops | bytes accessed | tf_op | source)
XLA Modules:
  0.0 114.1 jit_solution(16638673149675178397)
XLA Ops:
  0.6 1.9 %dispatch.1 = bf16[8,4,8320]{2,1,0:T(4,128)(2,1)S(1)} custom-call(s32[2,128]{1,0:T(2,128)} %bitcast.17, bf16[2,128]{1,0:T(2,128)(2,1)} %bitcast.20, bf16[128,4096]{1,0:T(8,128)(2,1)} %tok_hbm.1, bf16[128,4096]{1,0:T(8,128)(2,1)} %cot_hbm.1), custom_call_target="tpu_custom_call" | custom-call | tf_op jit(solution)/shard_map/dispatch/pallas_call | solution.py:301
  2.6 15.5 %all_to_all.16.in_ref = bf16[8,4,8320]{2,1,0:T(4,128)(2,1)S(1)} all-to-all(bf16[8,4,8320]{2,1,0:T(4,128)(2,1)S(1)} %dispatch.1), channel_id=1, replica_groups=mesh['x'=4,'zh'=4,'c'=2,'y'=4,'zl'=2] {'y','zl'}, dimensions={0} | all-to-all | bytes 1064960 | tf_op jit(solution)/shard_map/all_to_all | solution.py:316
  18.0 0.5 compact.1
  18.5 5.2 %collective-permute-start.5 = (bf16[16,8320]{1,0:T(8,128)(2,1)S(1)}, bf16[16,8320]{1,0:T(8,128)(2,1)S(1)}, u32[]{:S(2)}, u32[]{:S(2)}) collective-permute-start(bf16[16,8320]{1,0:T(8,128)(2,1)S(1)} %compact.1), channel_id=1, source_target_pairs={{0,48},{16,0},{32,16},{48,32},{1,49},{17,1},{33,17},{49,33},{2,50}... | collective-permute-start | bytes 798728 | tf_op jit(solution)/shard_map/ppermute | solution.py:289
  23.7 0.0 collective-permute-start.4
  23.7 2.7 %collective-permute-start.2 = (bf16[16,8320]{1,0:T(8,128)(2,1)S(1)}, bf16[16,8320]{1,0:T(8,128)(2,1)S(1)}, u32[]{:S(2)}, u32[]{:S(2)}) collective-permute-start(bf16[16,8320]{1,0:T(8,128)(2,1)S(1)} %compact.1), channel_id=1, source_target_pairs={{0,128},{64,192},{128,0},{192,64},{1,129},{65,193},{129,1},{193,65... | collective-permute-start | bytes 798728 | tf_op jit(solution)/shard_map/ppermute | solution.py:289
  26.4 0.9 collective-permute-start.1
  27.3 0.6 collective-permute-start
  27.9 6.0 %collective-permute-done.5 = bf16[16,8320]{1,0:T(8,128)(2,1)S(1)} collective-permute-done((bf16[16,8320]{1,0:T(8,128)(2,1)S(1)}, bf16[16,8320]{1,0:T(8,128)(2,1)S(1)}, u32[]{:S(2)}, u32[]{:S(2)}) %collective-permute-start.5) | collective-permute-done | bytes 266272 | tf_op jit(solution)/shard_map/ppermute | solution.py:289
  34.0 2.5 %collective-permute-done.4 = bf16[16,8320]{1,0:T(8,128)(2,1)S(1)} collective-permute-done((bf16[16,8320]{1,0:T(8,128)(2,1)S(1)}, bf16[16,8320]{1,0:T(8,128)(2,1)S(1)}, u32[]{:S(2)}, u32[]{:S(2)}) %collective-permute-start.4) | collective-permute-done | bytes 266272 | tf_op jit(solution)/shard_map/ppermute | solution.py:289
  36.5 0.0 collective-permute-done.2
  36.5 1.2 %collective-permute-done.1 = bf16[16,8320]{1,0:T(8,128)(2,1)S(1)} collective-permute-done((bf16[16,8320]{1,0:T(8,128)(2,1)S(1)}, bf16[16,8320]{1,0:T(8,128)(2,1)S(1)}, u32[]{:S(2)}, u32[]{:S(2)}) %collective-permute-start.1) | collective-permute-done | bytes 266272 | tf_op jit(solution)/shard_map/ppermute | solution.py:289
  37.7 0.0 collective-permute-done
  37.8 3.4 %collective-permute-start.7 = (bf16[32,8320]{1,0:T(8,128)(2,1)S(1)}, bf16[32,8320]{1,0:T(8,128)(2,1)S(1)}, u32[]{:S(2)}, u32[]{:S(2)}) collective-permute-start(bf16[32,8320]{1,0:T(8,128)(2,1)S(1)} %pad_maximum_fusion.1), channel_id=1, source_target_pairs={{0,192},{64,0},{128,64},{192,128},{1,193},{65,1},{129,65},{193,129... | collective-permute-start | bytes 1597448 | tf_op jit(solution)/shard_map/ppermute | solution.py:289
  41.2 0.0 collective-permute-start.6
  41.2 3.0 %collective-permute-start.8 = (bf16[16,8320]{1,0:T(8,128)(2,1)S(1)}, bf16[16,8320]{1,0:T(8,128)(2,1)S(1)}, u32[]{:S(2)}, u32[]{:S(2)}) collective-permute-start(bf16[16,8320]{1,0:T(8,128)(2,1)S(1)} %compact.1), channel_id=1, source_target_pairs={{0,32},{16,48},{32,0},{48,16},{1,33},{17,49},{33,1},{49,17},{2,34}... | collective-permute-start | bytes 798728 | tf_op jit(solution)/shard_map/ppermute | solution.py:289
  44.1 0.1 pad_maximum_fusion.refs_0_
  44.3 2.0 %collective-permute-start.3 = (bf16[64,8320]{1,0:T(8,128)(2,1)S(1)}, bf16[64,8320]{1,0:T(8,128)(2,1)S(1)}, u32[]{:S(2)}, u32[]{:S(2)}) collective-permute-start(bf16[64,8320]{1,0:T(8,128)(2,1)S(1)} %pad_maximum_fusion.refs_0_), channel_id=1, source_target_pairs={{0,8},{8,0},{1,9},{9,1},{2,10},{10,2},{3,11},{11,3},{4,12},{12,4},... | collective-permute-start | bytes 3194888 | tf_op jit(solution)/shard_map/ppermute | solution.py:289
  46.2 5.3 %collective-permute-done.7 = bf16[32,8320]{1,0:T(8,128)(2,1)S(1)} collective-permute-done((bf16[32,8320]{1,0:T(8,128)(2,1)S(1)}, bf16[32,8320]{1,0:T(8,128)(2,1)S(1)}, u32[]{:S(2)}, u32[]{:S(2)}) %collective-permute-start.7) | collective-permute-done | bytes 532512 | tf_op jit(solution)/shard_map/ppermute | solution.py:289
  51.5 0.2 collective-permute-done.8
  51.7 3.3 %collective-permute-start.12 = (bf16[32,8320]{1,0:T(8,128)(2,1)S(1)}, bf16[32,8320]{1,0:T(8,128)(2,1)S(1)}, u32[]{:S(2)}, u32[]{:S(2)}) collective-permute-start(bf16[32,8320]{1,0:T(8,128)(2,1)S(1)} %pad_maximum_fusion.3), channel_id=1, source_target_pairs={{0,192},{64,0},{128,64},{192,128},{1,193},{65,1},{129,65},{193,129... | collective-permute-start | bytes 1597448 | tf_op jit(solution)/shard_map/ppermute | solution.py:289
  55.0 0.0 collective-permute-done.6
  55.0 3.9 %collective-permute-start.13 = (bf16[16,8320]{1,0:T(8,128)(2,1)S(1)}, bf16[16,8320]{1,0:T(8,128)(2,1)S(1)}, u32[]{:S(2)}, u32[]{:S(2)}) collective-permute-start(bf16[16,8320]{1,0:T(8,128)(2,1)S(1)} %collective-permute-done.2), channel_id=1, source_target_pairs={{0,32},{16,48},{32,0},{48,16},{1,33},{17,49},{33,1},{49,17},{2,34}... | collective-permute-start | bytes 798728 | tf_op jit(solution)/shard_map/ppermute | solution.py:289
  58.9 0.0 copy-start.2
  59.0 0.0 copy-start
  59.0 0.0 copy-start.1
  59.0 3.6 %collective-permute-start.9 = (bf16[112,8320]{1,0:T(8,128)(2,1)S(1)}, bf16[112,8320]{1,0:T(8,128)(2,1)S(1)}, u32[]{:S(2)}, u32[]{:S(2)}) collective-permute-start(bf16[112,8320]{1,0:T(8,128)(2,1)S(1)} %constant_dynamic-update-slice_fusion.refs_2_), channel_id=1, source_target_pairs={{0,8},{8,0},{1,9},{9,1},{2,10},{10,2},{3,11},{11,3},{4,12},{12,4},... | collective-permute-start | bytes 5591048 | tf_op jit(solution)/shard_map/ppermute | solution.py:289
  62.7 0.8 collective-permute-done.12
  63.6 0.0 collective-permute-done.3.refs_1_
  63.6 0.1 pad_maximum_fusion.2
  63.6 0.7 collective-permute-start.10
  64.3 0.1 collective-permute-done.13
  64.5 4.5 %collective-permute-start.14 = (bf16[48,8320]{1,0:T(8,128)(2,1)S(1)}, bf16[48,8320]{1,0:T(8,128)(2,1)S(1)}, u32[]{:S(2)}, u32[]{:S(2)}) collective-permute-start(bf16[48,8320]{1,0:T(8,128)(2,1)S(1)} %constant_dynamic-update-slice_fusion.4.refs_3_), channel_id=1, source_target_pairs={{0,8},{8,0},{1,9},{9,1},{2,10},{10,2},{3,11},{11,3},{4,12},{12,4},... | collective-permute-start | bytes 2396168 | tf_op jit(solution)/shard_map/ppermute | solution.py:289
  68.9 0.0 collective-permute-done.9.refs_3_.refs_0_
  68.9 0.0 copy-done.2
  68.9 0.0 copy-done
  68.9 0.0 copy-done.1
  68.9 6.1 %first.1 = (f32[8,256]{1,0:T(8,128)S(1)}, bf16[3,224,4096]{2,1,0:T(8,128)(2,1)}, bf16[96,8320]{1,0:T(8,128)(2,1)}) custom-call(bf16[64,8320]{1,0:T(8,128)(2,1)S(1)} %pad_maximum_fusion.refs_0_, bf16[64,8320]{1,0:T(8,128)(2,1)S(1)} %collective-permute-done.3.refs_1_, bf16[112,8320]{1,0:T(8,128)(2,1)S(1)} %constant_dynamic-update-slice_fusion.refs_2_, ...), custom_call_target="tpu_custom_call" | custom-call | tf_op jit(solution)/shard_map/first/pallas_call | solution.py:356
  75.0 0.7 collective-permute-done.10.refs_1_
  75.7 4.5 %collective-permute-start.11 = (bf16[32,8320]{1,0:T(8,128)(2,1)S(1)}, bf16[32,8320]{1,0:T(8,128)(2,1)S(1)}, u32[]{:S(2)}, u32[]{:S(2)}) collective-permute-start(bf16[32,8320]{1,0:T(8,128)(2,1)S(1)} %collective-permute-done.10.refs_1_), channel_id=1, source_target_pairs={{0,8},{8,0},{1,9},{9,1},{2,10},{10,2},{3,11},{11,3},{4,12},{12,4},... | collective-permute-start | bytes 1597448 | tf_op jit(solution)/shard_map/ppermute | solution.py:289
  80.2 0.0 collective-permute-done.14.refs_4_
  80.2 1.5 %collective-permute-done.11.refs_2_ = bf16[32,8320]{1,0:T(8,128)(2,1)S(1)} collective-permute-done((bf16[32,8320]{1,0:T(8,128)(2,1)S(1)}, bf16[32,8320]{1,0:T(8,128)(2,1)S(1)}, u32[]{:S(2)}, u32[]{:S(2)}) %collective-permute-start.11) | collective-permute-done | bytes 532512 | tf_op jit(solution)/shard_map/ppermute | solution.py:289
  81.7 3.9 %last.1 = (bf16[160,8320]{1,0:T(8,128)(2,1)}, bf16[3,224,256]{2,1,0:T(8,128)(2,1)}, f32[256,128]{1,0:T(8,128)}) custom-call(bf16[112,8320]{1,0:T(8,128)(2,1)S(1)} %collective-permute-done.9.refs_3_.refs_0_, bf16[32,8320]{1,0:T(8,128)(2,1)S(1)} %collective-permute-done.10.refs_1_, bf16[32,8320]{1,0:T(8,128)(2,1)S(1)} %collective-permute-done.11.refs_2_, ...), custom_call_target="tpu_custom_call" | custom-call | tf_op jit(solution)/shard_map/last/pallas_call | solution.py:379
  85.6 14.8 %all-to-all-start.1 = ((f32[256,1,128]{2,1,0:T(1,128)}), f32[256,1,128]{2,1,0:T(1,128)S(1)}, u32[]{:S(2)}, u32[]{:S(2)}) async-start(f32[256,1,128]{2,1,0:T(1,128)} %bitcast.6), calls=%async_computation.1 | async-start | bytes 262144 | tf_op jit(solution)/shard_map/all_to_all | solution.py:395
  100.4 0.0 copy-start.3
  100.4 7.4 %backward.1 = (bf16[1,224,4096]{2,1,0:T(8,128)(2,1)}, bf16[1,224,4096]{2,1,0:T(8,128)(2,1)}, bf16[1,224,4096]{2,1,0:T(8,128)(2,1)}) custom-call(bf16[96,8320]{1,0:T(8,128)(2,1)} %get-tuple-element.20.left_hbm, bf16[160,8320]{1,0:T(8,128)(2,1)} %get-tuple-element.25.rows_hbm, bf16[3,224,256]{2,1,0:T(8,128)(2,1)} %get-tuple-element.26.fact_hbm, ...), custom_call_target="tpu_custom_call" | custom-call | tf_op jit(solution)/shard_map/backward/pallas_call | solution.py:397
  107.8 5.6 %all-to-all-done.1 = f32[256,1,128]{2,1,0:T(1,128)S(1)} async-done(((f32[256,1,128]{2,1,0:T(1,128)}), f32[256,1,128]{2,1,0:T(1,128)S(1)}, u32[]{:S(2)}, u32[]{:S(2)}) %all-to-all-start.1) | async-done | bytes 131104 | tf_op jit(solution)/shard_map/all_to_all | solution.py:395
  113.4 0.0 copy-done.3
  113.4 0.7 collect.1
  (10 shorter events, 0.3 us)
Async XLA Ops:
  18.5 15.5 %collective-permute-start.5 = (bf16[16,8320]{1,0:T(8,128)(2,1)S(1)}, bf16[16,8320]{1,0:T(8,128)(2,1)S(1)}, u32[]{:S(2)}, u32[]{:S(2)}) collective-permute-start(bf16[16,8320]{1,0:T(8,128)(2,1)S(1)} %compact.1), channel_id=1, source_target_pairs={{0,48},{16,0},{32,16},{48,32},{1,49},{17,1},{33,17},{49,33},{2,50}... | collective-permute-start | bytes 798728 | tf_op jit(solution)/shard_map/ppermute | solution.py:289
  23.7 12.8 %collective-permute-start.4 = (bf16[16,8320]{1,0:T(8,128)(2,1)S(1)}, bf16[16,8320]{1,0:T(8,128)(2,1)S(1)}, u32[]{:S(2)}, u32[]{:S(2)}) collective-permute-start(bf16[16,8320]{1,0:T(8,128)(2,1)S(1)} %compact.1), channel_id=1, source_target_pairs={{0,16},{16,32},{32,48},{48,0},{1,17},{17,33},{33,49},{49,1},{2,18}... | collective-permute-start | bytes 798728 | tf_op jit(solution)/shard_map/ppermute | solution.py:289
  23.7 12.8 %collective-permute-start.2 = (bf16[16,8320]{1,0:T(8,128)(2,1)S(1)}, bf16[16,8320]{1,0:T(8,128)(2,1)S(1)}, u32[]{:S(2)}, u32[]{:S(2)}) collective-permute-start(bf16[16,8320]{1,0:T(8,128)(2,1)S(1)} %compact.1), channel_id=1, source_target_pairs={{0,128},{64,192},{128,0},{192,64},{1,129},{65,193},{129,1},{193,65... | collective-permute-start | bytes 798728 | tf_op jit(solution)/shard_map/ppermute | solution.py:289
  26.4 11.3 %collective-permute-start.1 = (bf16[16,8320]{1,0:T(8,128)(2,1)S(1)}, bf16[16,8320]{1,0:T(8,128)(2,1)S(1)}, u32[]{:S(2)}, u32[]{:S(2)}) collective-permute-start(bf16[16,8320]{1,0:T(8,128)(2,1)S(1)} %compact.1), channel_id=1, source_target_pairs={{0,192},{64,0},{128,64},{192,128},{1,193},{65,1},{129,65},{193,129... | collective-permute-start | bytes 798728 | tf_op jit(solution)/shard_map/ppermute | solution.py:289
  27.3 10.5 %collective-permute-start = (bf16[16,8320]{1,0:T(8,128)(2,1)S(1)}, bf16[16,8320]{1,0:T(8,128)(2,1)S(1)}, u32[]{:S(2)}, u32[]{:S(2)}) collective-permute-start(bf16[16,8320]{1,0:T(8,128)(2,1)S(1)} %compact.1), channel_id=1, source_target_pairs={{0,64},{64,128},{128,192},{192,0},{1,65},{65,129},{129,193},{193,1... | collective-permute-start | bytes 798728 | tf_op jit(solution)/shard_map/ppermute | solution.py:289
  37.8 13.7 %collective-permute-start.7 = (bf16[32,8320]{1,0:T(8,128)(2,1)S(1)}, bf16[32,8320]{1,0:T(8,128)(2,1)S(1)}, u32[]{:S(2)}, u32[]{:S(2)}) collective-permute-start(bf16[32,8320]{1,0:T(8,128)(2,1)S(1)} %pad_maximum_fusion.1), channel_id=1, source_target_pairs={{0,192},{64,0},{128,64},{192,128},{1,193},{65,1},{129,65},{193,129... | collective-permute-start | bytes 1597448 | tf_op jit(solution)/shard_map/ppermute | solution.py:289
  41.2 13.9 %collective-permute-start.6 = (bf16[32,8320]{1,0:T(8,128)(2,1)S(1)}, bf16[32,8320]{1,0:T(8,128)(2,1)S(1)}, u32[]{:S(2)}, u32[]{:S(2)}) collective-permute-start(bf16[32,8320]{1,0:T(8,128)(2,1)S(1)} %pad_maximum_fusion.1), channel_id=1, source_target_pairs={{0,64},{64,128},{128,192},{192,0},{1,65},{65,129},{129,193},{193,1... | collective-permute-start | bytes 1597448 | tf_op jit(solution)/shard_map/ppermute | solution.py:289
  41.2 10.5 %collective-permute-start.8 = (bf16[16,8320]{1,0:T(8,128)(2,1)S(1)}, bf16[16,8320]{1,0:T(8,128)(2,1)S(1)}, u32[]{:S(2)}, u32[]{:S(2)}) collective-permute-start(bf16[16,8320]{1,0:T(8,128)(2,1)S(1)} %compact.1), channel_id=1, source_target_pairs={{0,32},{16,48},{32,0},{48,16},{1,33},{17,49},{33,1},{49,17},{2,34}... | collective-permute-start | bytes 798728 | tf_op jit(solution)/shard_map/ppermute | solution.py:289
  44.3 19.3 %collective-permute-start.3 = (bf16[64,8320]{1,0:T(8,128)(2,1)S(1)}, bf16[64,8320]{1,0:T(8,128)(2,1)S(1)}, u32[]{:S(2)}, u32[]{:S(2)}) collective-permute-start(bf16[64,8320]{1,0:T(8,128)(2,1)S(1)} %pad_maximum_fusion.refs_0_), channel_id=1, source_target_pairs={{0,8},{8,0},{1,9},{9,1},{2,10},{10,2},{3,11},{11,3},{4,12},{12,4},... | collective-permute-start | bytes 3194888 | tf_op jit(solution)/shard_map/ppermute | solution.py:289
  51.7 11.8 %collective-permute-start.12 = (bf16[32,8320]{1,0:T(8,128)(2,1)S(1)}, bf16[32,8320]{1,0:T(8,128)(2,1)S(1)}, u32[]{:S(2)}, u32[]{:S(2)}) collective-permute-start(bf16[32,8320]{1,0:T(8,128)(2,1)S(1)} %pad_maximum_fusion.3), channel_id=1, source_target_pairs={{0,192},{64,0},{128,64},{192,128},{1,193},{65,1},{129,65},{193,129... | collective-permute-start | bytes 1597448 | tf_op jit(solution)/shard_map/ppermute | solution.py:289
  55.0 9.4 %collective-permute-start.13 = (bf16[16,8320]{1,0:T(8,128)(2,1)S(1)}, bf16[16,8320]{1,0:T(8,128)(2,1)S(1)}, u32[]{:S(2)}, u32[]{:S(2)}) collective-permute-start(bf16[16,8320]{1,0:T(8,128)(2,1)S(1)} %collective-permute-done.2), channel_id=1, source_target_pairs={{0,32},{16,48},{32,0},{48,16},{1,33},{17,49},{33,1},{49,17},{2,34}... | collective-permute-start | bytes 798728 | tf_op jit(solution)/shard_map/ppermute | solution.py:289
  58.9 10.0 %copy-start.2 = (bf16[1,224,4096]{2,1,0:T(8,128)(2,1)S(1)}, bf16[1,224,4096]{2,1,0:T(8,128)(2,1)}, u32[]{:S(2)}) copy-start(bf16[1,224,4096]{2,1,0:T(8,128)(2,1)} %param.13) | copy-start | bytes 5505028
  59.0 9.9 %copy-start = (bf16[1,224,4096]{2,1,0:T(8,128)(2,1)S(1)}, bf16[1,224,4096]{2,1,0:T(8,128)(2,1)}, u32[]{:S(2)}) copy-start(bf16[1,224,4096]{2,1,0:T(8,128)(2,1)} %param.11) | copy-start | bytes 5505028
  59.0 9.9 %copy-start.1 = (bf16[1,224,4096]{2,1,0:T(8,128)(2,1)S(1)}, bf16[1,224,4096]{2,1,0:T(8,128)(2,1)}, u32[]{:S(2)}) copy-start(bf16[1,224,4096]{2,1,0:T(8,128)(2,1)} %param.12) | copy-start | bytes 5505028
  59.0 9.9 %collective-permute-start.9 = (bf16[112,8320]{1,0:T(8,128)(2,1)S(1)}, bf16[112,8320]{1,0:T(8,128)(2,1)S(1)}, u32[]{:S(2)}, u32[]{:S(2)}) collective-permute-start(bf16[112,8320]{1,0:T(8,128)(2,1)S(1)} %constant_dynamic-update-slice_fusion.refs_2_), channel_id=1, source_target_pairs={{0,8},{8,0},{1,9},{9,1},{2,10},{10,2},{3,11},{11,3},{4,12},{12,4},... | collective-permute-start | bytes 5591048 | tf_op jit(solution)/shard_map/ppermute | solution.py:289
  63.6 12.1 %collective-permute-start.10 = (bf16[32,8320]{1,0:T(8,128)(2,1)S(1)}, bf16[32,8320]{1,0:T(8,128)(2,1)S(1)}, u32[]{:S(2)}, u32[]{:S(2)}) collective-permute-start(bf16[32,8320]{1,0:T(8,128)(2,1)S(1)} %pad_maximum_fusion.2), channel_id=1, source_target_pairs={{0,64},{64,128},{128,192},{192,0},{1,65},{65,129},{129,193},{193,1... | collective-permute-start | bytes 1597448 | tf_op jit(solution)/shard_map/ppermute | solution.py:289
  64.5 15.7 %collective-permute-start.14 = (bf16[48,8320]{1,0:T(8,128)(2,1)S(1)}, bf16[48,8320]{1,0:T(8,128)(2,1)S(1)}, u32[]{:S(2)}, u32[]{:S(2)}) collective-permute-start(bf16[48,8320]{1,0:T(8,128)(2,1)S(1)} %constant_dynamic-update-slice_fusion.4.refs_3_), channel_id=1, source_target_pairs={{0,8},{8,0},{1,9},{9,1},{2,10},{10,2},{3,11},{11,3},{4,12},{12,4},... | collective-permute-start | bytes 2396168 | tf_op jit(solution)/shard_map/ppermute | solution.py:289
  75.7 6.0 %collective-permute-start.11 = (bf16[32,8320]{1,0:T(8,128)(2,1)S(1)}, bf16[32,8320]{1,0:T(8,128)(2,1)S(1)}, u32[]{:S(2)}, u32[]{:S(2)}) collective-permute-start(bf16[32,8320]{1,0:T(8,128)(2,1)S(1)} %collective-permute-done.10.refs_1_), channel_id=1, source_target_pairs={{0,8},{8,0},{1,9},{9,1},{2,10},{10,2},{3,11},{11,3},{4,12},{12,4},... | collective-permute-start | bytes 1597448 | tf_op jit(solution)/shard_map/ppermute | solution.py:289
  85.6 27.8 %all-to-all-start.1 = ((f32[256,1,128]{2,1,0:T(1,128)}), f32[256,1,128]{2,1,0:T(1,128)S(1)}, u32[]{:S(2)}, u32[]{:S(2)}) async-start(f32[256,1,128]{2,1,0:T(1,128)} %bitcast.6), calls=%async_computation.1 | async-start | bytes 262144 | tf_op jit(solution)/shard_map/all_to_all | solution.py:395
  100.4 13.0 %copy-start.3 = (s32[128,2]{0,1:T(2,128)S(1)}, s32[128,2]{0,1:T(2,128)}, u32[]{:S(2)}) copy-start(s32[128,2]{0,1:T(2,128)} %param.9) | copy-start | bytes 3076
